TPU v7x, 512 devices: a whole 4x8x8 slice. The times are simulated.
512 devices in a mesh: ka: 8 (over y_hi, core), pb: 16 (over y_lo, z), row: 4 (over x).
Axes of the slice: x: 4, y: 8 (y_hi: 4, y_lo: 2; y = y_hi * 2 + y_lo), z: 8, core: 2. Of those that a mesh axis runs over, the one named last changes fastest.
Arguments:
- coupling: bfloat16 [64, 64, 20736], P('pb', ('ka', 'row')), may hold values from -1 to 1
- rotation: bfloat16 [64, 36, 36], P('pb'), may hold values from -1 to 1
- freq: float32 [64, 36], P('pb'), may hold values from 0.02 to 0.3
- eigvec: bfloat16 [1024, 24, 24], P(('ka', 'row')), may hold values from -1.25 to 1.25
- energies: float32 [1024, 24], P(('ka', 'row')), may hold values from -1.5 to 1.5
- window: int32 [1024], P(('ka', 'row')), may hold values from 12 to 24
- kq_index: int32 [64, 1024], P('pb'), may hold values from 0 to 1023, as said below
- kpoints: float32 [1024, 3], replicated, may hold values from 0 to 1
- lattice: int32 [64, 3], replicated, may hold values from -3 to 3
Outputs:
- electron: float32 [1024, 24], P(('ka', 'row'))
- phonon: float32 [64, 36], P('pb')
Inputs may be any that keep to these rules, and one draw needn't show every extreme that they name: The k-points form a shifted grid of 1024 points, (1024 // 64) x 8 x 8, listed in an order drawn from the seed; each q-point is a vector of that grid without the shift. kq_index[q, k] is the index of the k-point equal to kpoints[k] plus the q-point's vector modulo 1, so each row of kq_index is a permutation of 0 to 1023.
All inputs are finite; a program needn't handle non-finite values.
Results may differ from a plain program's by a relative error of at most 0.00089.
Values may be sent and summed in bfloat16 or wider, within the bound.
A program may use at most 128 MiB of HBM per device.

v0:
```python
import math

import jax
import jax.numpy as jnp
from jax import lax
from jax.sharding import PartitionSpec as P

SIGMA = 0.1
THERMAL_ENERGY_KT = 0.2


def phase_table(lattice, kpoint_rows):
    rvec = lattice.astype(jnp.float32)
    argument = (
        rvec[:, 0:1] * kpoint_rows[:, 0][None, :]
        + rvec[:, 1:2] * kpoint_rows[:, 1][None, :]
        + rvec[:, 2:3] * kpoint_rows[:, 2][None, :]
    )
    return jnp.cos(2.0 * math.pi * argument).astype(jnp.bfloat16)


def block_terms(
    coup_rows, phase_cols, rot_rows, freq_rows, eig_k, eig_kq, level_k, level_kq, lim_k, lim_kq
):
    q_block = coup_rows.shape[0]
    k_block = phase_cols.shape[1]
    columns = q_block * k_block
    n_modes = rot_rows.shape[1]
    n_bands = eig_k.shape[0]
    norm = 1.0 / (math.sqrt(2.0 * math.pi) * SIGMA)
    bloch = jnp.einsum(
        "qrf,rk->fqk", coup_rows, phase_cols, preferred_element_type=jnp.float32
    ).astype(jnp.bfloat16)
    bloch = bloch.reshape(n_modes, n_bands, n_bands, columns)
    rot_cols = jnp.repeat(jnp.transpose(rot_rows, (1, 2, 0)), k_block, axis=2)
    modal = jnp.einsum(
        "amnc,abc->bmnc", bloch, rot_cols, preferred_element_type=jnp.float32
    ).astype(jnp.bfloat16)
    eig_k_cols = jnp.tile(eig_k, (1, 1, q_block))
    right = jnp.einsum(
        "bmjc,jnc->bmnc", modal, eig_k_cols, preferred_element_type=jnp.float32
    ).astype(jnp.bfloat16)
    coupled = jnp.einsum("imc,binc->bmnc", eig_kq, right, preferred_element_type=jnp.float32)
    level_k_cols = jnp.tile(level_k, (1, q_block))
    lim_k_cols = jnp.tile(lim_k, (q_block,))
    freq_cols = jnp.repeat(freq_rows.T, k_block, axis=1)
    diff = level_kq[None, :, None, :] - level_k_cols[None, None, :, :] - freq_cols[:, None, None, :]
    delta = jnp.exp(-(diff * diff) / (2.0 * SIGMA * SIGMA)) * norm
    bands = jnp.arange(n_bands).astype(jnp.float32)
    mask_m = (bands[:, None] < lim_kq[None, :]).astype(jnp.float32)
    mask_n = (bands[:, None] < lim_k_cols[None, :]).astype(jnp.float32)
    strength = coupled * coupled * delta * mask_m[None, :, None, :] * mask_n[None, None, :, :]
    filling_initial = jax.nn.sigmoid(-level_k_cols / THERMAL_ENERGY_KT)
    filling_final = jax.nn.sigmoid(-level_kq / THERMAL_ENERGY_KT)
    elec = jnp.sum(strength, axis=(0, 1)).reshape(n_bands, q_block, k_block).sum(axis=1)
    phon = jnp.sum(
        strength * (filling_initial[None, None, :, :] - filling_final[None, :, None, :]),
        axis=(1, 2),
    )
    phon = phon.reshape(n_modes, q_block, k_block).sum(axis=2)
    return (elec, phon)


def on_device(coupling, rotation, freq, eigvec, energies, window, kq_index, kpoints, lattice):
    n_ka = lax.axis_size("ka")
    n_row = lax.axis_size("row")
    n_pb = lax.axis_size("pb")
    k_dev = eigvec.shape[0]
    q_dev = rotation.shape[0]
    n_bands = eigvec.shape[1]
    n_modes = rotation.shape[1]
    total_k = k_dev * n_ka * n_row
    total_q = q_dev * n_pb
    eigen_grid = lax.all_gather(eigvec, ("ka", "row"), axis=0, tiled=True)
    level_all, limit_all = (
        lax.all_gather(energies, ("ka", "row"), axis=0, tiled=True),
        lax.all_gather(window.astype(jnp.float32), ("ka", "row"), axis=0, tiled=True),
    )
    eig_cols = jnp.transpose(eigen_grid, (1, 2, 0))
    level_cols = level_all.T
    ka_pos = lax.axis_index("ka")
    row_pos = lax.axis_index("row")
    coup_full = lax.all_gather(coupling, ("ka", "row"), axis=1, tiled=True)
    q_start = jnp.int32(0)
    k_start = (ka_pos * n_row + row_pos) * k_dev
    kq_mine = lax.dynamic_slice(kq_index, (q_start, k_start), (q_dev, k_dev))
    kp_mine = lax.dynamic_slice(kpoints, (k_start, jnp.int32(0)), (k_dev, 3))
    eig_mine = lax.dynamic_slice_in_dim(eig_cols, k_start, k_dev, 2)
    lev_mine = lax.dynamic_slice_in_dim(level_cols, k_start, k_dev, 1)
    lim_mine = lax.dynamic_slice_in_dim(limit_all, k_start, k_dev, 0)
    phase_all = phase_table(lattice, kp_mine)
    k_block = min(k_dev, 128)
    elec_cols = [None] * (k_dev // k_block)
    index = kq_mine.reshape(-1)
    eig_kq = jnp.take(eig_cols, index, axis=2)
    level_kq = jnp.take(level_cols, index, axis=1)
    lim_kq = jnp.take(limit_all, index, axis=0)
    elec, phon = block_terms(
        coup_full, phase_all, rotation, freq, eig_mine, eig_kq, lev_mine, level_kq, lim_mine, lim_kq
    )
    elec_cols[0] = elec
    elec_local = elec_cols[0].T * (1.0 / (total_q * n_modes * n_bands))
    phon_local = phon.T * (1.0 / (total_k * n_bands))
    phonon = lax.psum(phon_local, ("ka", "row"))
    electron = lax.psum(elec_local, "pb")
    return (electron, phonon)


def solution(mesh):
    return jax.shard_map(
        on_device,
        mesh=mesh,
        in_specs=(
            P("pb", ("ka", "row"), None),
            P("pb", None, None),
            P("pb", None),
            P(("ka", "row"), None, None),
            P(("ka", "row"), None),
            P(("ka", "row")),
            P("pb", None),
            P(),
            P(),
        ),
        out_specs=(P(("ka", "row"), None), P("pb", None)),
        check_vma=False,
    )
```

profile of v0, /device:TPU:1, one launch (start us, length us, event | category | flops | bytes accessed | tf_op | source)
XLA Modules:
  0.0 543.8 jit_solution(66930285304489676)
XLA Ops:
  7.2 1.7 copy.47
  9.0 1.8 copy.49
  11.2 0.7 convert_element_type.50
  11.8 1.3 dynamic-slice.8
  13.8 0.8 convert_dynamic-update-slice_fusion
  14.5 73.2 %all-reduce = f32[1024]{0:T(1024)S(1)} all-reduce(f32[1024]{0:T(1024)S(1)} %convert_dynamic-update-slice_fusion), channel_id=1, replica_groups=mesh['ka'=8,'pb'=16,'row'=4] {'ka','row'}, use_global_device_ids=true, to_apply=%add | all-reduce | flops 1024 | bytes 8192
  87.9 1.0 gather_fusion.2
  89.0 0.8 copy.79
  89.8 0.1 copy.62
  90.0 79.1 %all-gather = f32[32,32,24]{1,2,0:T(8,128)S(1)} all-gather(f32[1,32,24]{1,2,0:T(8,128)} %bitcast.93), channel_id=1, replica_groups=mesh['ka'=8,'pb'=16,'row'=4] {'ka','row'}, dimensions={0}, use_global_device_ids=true | all-gather | bytes 101376 | tf_op jit(solution)/shard_map/all_gather | solution.py:76
  169.2 0.2 copy.57
  169.6 0.1 copy.61
  169.7 0.1 copy.64
  169.8 0.7 gather_fusion.1
  170.6 0.1 copy.65
  170.8 0.8 constant_dynamic-slice_fusion.1
  171.5 2.1 broadcast_subtract_fusion
  173.6 1.0 dynamic-slice_bitcast_fusion
  174.6 0.1 copy.48
  174.7 3.7 gather_fusion
  178.4 8.7 %all-gather.6.cloned.1.call-done = bf16[4,64,20736]{2,0,1:T(4,128)(2,1)} async-done(((bf16[4,2,20736]{2,0,1:T(4,128)(2,1)}), bf16[4,64,20736]{2,0,1:T(4,128)(2,1)}) %all-gather.6.cloned.1.call-update) | async-done | bytes 10616848 | tf_op jit(solution)/shard_map/all_gather | solution.py:83
  187.1 8.0 %fusion.4 = bf16[20736,4,32]{0,2,1:T(8,128)(2,1)} fusion(bf16[4,64,20736]{2,0,1:T(4,128)(2,1)} %all-gather.6.cloned.1.call-done, f32[32]{0:T(128)S(1)} %get-tuple-element.18, f32[64]{0:T(128)S(1)} %get-tuple-element.15, f32[32]{0:T(128)S(1)} %get-tuple-element.19, f32[64]{0:T(128)S(1)} %get-tuple-element.16, f32[32]{0:T(128)S(1)} %get-tuple-element.17, ...), kind=kOutput, calls=%fused_computation.10 | convolution fusion | flops 342407168 | bytes 15926400 | tf_op jit(solution)/shard_map/qrf,rk->fqk/dot_general | solution.py:31
  195.1 47.2 %reshape.253 = bf16[36,24,24,128]{2,1,0,3:T(8,128)(2,1)} reshape(bf16[20736,4,32]{0,2,1:T(8,128)(2,1)} %fusion.4) | data formatting | bytes 10616832 | tf_op jit(solution)/shard_map/reshape | solution.py:34
  242.4 0.1 tile.10
  242.5 0.2 broadcast_in_dim.40.clone
  242.6 23.3 %convert_bitcast_fusion = bf16[36,24,24,128]{0,2,1,3:T(8,128)(2,1)} fusion(bf16[24,24,128,1]{0,1,3,2:T(8,128)(2,1)S(1)} %bitcast.86, bf16[36,36,128,1]{1,0,3,2:T(8,128)(2,1)S(1)} %bitcast.85, bf16[36,24,24,128]{2,1,0,3:T(8,128)(2,1)} %reshape.253), kind=kOutput, calls=%fused_computation.15 | convolution fusion | flops 323813376 | bytes 11096064 | tf_op jit(solution)/shard_map/bmjc,jnc->bmnc/dot_general | solution.py:40
  266.0 69.3 %multiply_reduce_fusion = (f32[36,128]{0,1:T(8,128)S(1)}, f32[24,128]{0,1:T(8,128)S(1)}) fusion(f32[24,24,128]{0,1,2:T(8,128)} %get-tuple-element.22, f32[24,128]{0,1:T(8,128)S(1)} %copy.63, f32[24,128]{0,1:T(8,128)S(1)} %copy.62, f32[36,128]{0,1:T(8,128)S(1)} %bitcast.90, f32[24,24,128]{0,1,2:T(8,128)} %get-tuple-element.23, ...), kind=kOutput, calls=%fused_computation.6 | convolution fusion | flops 159318528 | bytes 6119552 | tf_op jit(solution)/shard_map/imc,binc->bmnc/dot_general | solution.py:43
  335.3 51.5 %psum.14 = f32[32,24]{1,0:T(8,128)S(1)} all-reduce(f32[32,24]{1,0:T(8,128)S(1)} %multiply_bitcast_fusion.1), channel_id=1, replica_groups=mesh['ka'=8,'pb'=16,'row'=4] {'pb'}, use_global_device_ids=true, to_apply=%region_2.3 | all-reduce | flops 768 | bytes 6144 | tf_op jit(solution)/shard_map/psum | solution.py:105
  386.8 0.7 copy.67
  387.5 0.1 copy.78
  387.6 148.7 %psum.15 = f32[4,36]{0,1:T(8,128)S(1)} all-reduce(f32[4,36]{0,1:T(8,128)S(1)} %multiply_bitcast_fusion), channel_id=1, replica_groups=mesh['ka'=8,'pb'=16,'row'=4] {'ka','row'}, use_global_device_ids=true, to_apply=%region_5.6 | all-reduce | flops 144 | bytes 1152 | tf_op jit(solution)/shard_map/psum | solution.py:104
  536.3 0.7 copy.68
  (39 shorter events, 1.2 us)
Async XLA Ops:
  7.2 3.7 copy-start
  7.2 166.5 %all-gather.4.cloned.1.call-start = ((), (), s32[]{:S(2)}) async-start(), calls=%async_computation | async-start | bytes 6488064 | tf_op jit(solution)/shard_map/all_gather | solution.py:74
  9.0 178.1 %all-gather.6.cloned.1.call-start = ((), (), s32[]{:S(2)}) async-start(), calls=%async_computation.1 | async-start | bytes 10948608 | tf_op jit(solution)/shard_map/all_gather | solution.py:83
  242.6 23.3 %copy-start.2 = (f32[4,36]{1,0:T(4,128)S(1)}, f32[4,36]{1,0:T(4,128)}, u32[]{:S(2)}) copy-start(f32[4,36]{1,0:T(4,128)} %param.11) | copy-start | bytes 1732
  265.9 271.0 %copy-start.1 = (s32[4,1024]{1,0:T(4,128)S(1)}, s32[4,1024]{1,0:T(4,128)}, u32[]{:S(2)}) copy-start(s32[4,1024]{1,0:T(4,128)} %param.15) | copy-start | bytes 49156
Sparse Core Ops, SparseCore 0:
  11.1 80.1 all-gather.3
  94.4 92.6 all-gather.5
where the time goes:
time: 555 us; the launch traced here: 544 us
  blocking collectives  353 us (64%)
  matrix products  101 us (18%)
  local copies, waits for them, and re-layouts  63.2 us (11%)
  between operations  14.9 us (3%)
  waiting for transfers between devices  8.77 us (2%)
    psum x1, blocking collectives, on_device(): phonon = lax.psum(phon_local, ('ka', 'row'))  149 us
    all_gather x1, blocking collectives, on_device(): lax.all_gather(energies, ('ka', 'row'), axis=0, tiled=True)  79.1 us
    unnamed x1, blocking collectives  73.2 us
    dot_general x1, matrix products, block_terms(): jnp.einsum('imc,binc->bmnc', eig_kq, right, preferred_element_type=jnp.fl...  69.3 us
    psum x1, blocking collectives, on_device(): electron = lax.psum(elec_local, 'pb')  51.5 us
    reshape x1, local copies, waits for them, and re-layouts, block_terms(): bloch = bloch.reshape(n_modes, n_bands, n_bands, columns)  47.2 us
    dot_general x1, matrix products, block_terms(): jnp.einsum('bmjc,jnc->bmnc', modal, eig_k_cols, preferred_element_type=jn...  23.3 us
  transfers between devices with their start and end apart: 2, of which 1 were waited for; matrix products, arithmetic and copies ran while one was open for 3% of the time, Pallas kernels for 0%

commit v1 on v0

v1 whole, which is shorter than its diff:
```python
import math

import jax
import jax.numpy as jnp
from jax import lax
from jax.sharding import PartitionSpec as P
from jax.experimental import pallas as pl
from jax.experimental.pallas import tpu as pltpu

SIGMA = 0.1
KT = 0.2
NB, NM, NR = 24, 36, 64
NV = 9
PITCH = 32
BLOCK = 32
TILES = 8
VSLOT = [(v // 5, v % 5) for v in range(NV)]


def compute_kernel(core_ref, kq_ref, freq_ref, phase_ref, rt_ref, eig_ref, etab_ref, el_ref,
                   tab, etile, pscr, etscr, ektscr, wscr, xscr, bd, ybuf, aescr, phacc):
    f32, bf16 = jnp.float32, jnp.bfloat16
    core = core_ref[0]
    lane = lax.broadcasted_iota(jnp.int32, (1, 128), 1)
    slot_lane = lane % PITCH

    row = lax.broadcasted_iota(jnp.int32, (128, 128), 0)
    col = lax.broadcasted_iota(jnp.int32, (128, 128), 1)
    pick = jnp.where((row % PITCH == NB) & (row // PITCH == col // PITCH), 1.0, 0.0).astype(bf16)
    lim = jnp.dot(etab_ref[...].astype(bf16), pick, preferred_element_type=f32)
    etile[...] = jnp.where(slot_lane.astype(f32) < lim, 1.0, 0.0)

    def build_table(t, _):
        m = etile[pl.ds((t % 32) * TILES + t // 32, 1), :]
        tab[t] = eig_ref[t].astype(f32) * m
        return 0
    lax.fori_loop(0, 256, build_table, 0, unroll=8)

    r1 = lax.broadcasted_iota(jnp.int32, (NB, 384), 0)
    c1 = lax.broadcasted_iota(jnp.int32, (NB, 384), 1)
    spread = jnp.where(c1 % NB == r1, 1.0, 0.0).astype(bf16)
    r2 = lax.broadcasted_iota(jnp.int32, (NR, NR * NB), 0)
    c2 = lax.broadcasted_iota(jnp.int32, (NR, NR * NB), 1)
    widen = jnp.where(c2 // NB == r2, 1.0, 0.0).astype(bf16)
    r3 = lax.broadcasted_iota(jnp.int32, (256, 128), 0)
    c3 = lax.broadcasted_iota(jnp.int32, (256, 128), 1)
    fold = jnp.where(r3 // PITCH == c3, 1.0, 0.0).astype(f32)

    pscr[...] = jnp.dot(phase_ref[...], widen, preferred_element_type=f32)
    for ch in range(16):
        blk = core * 16 + ch
        ektscr[ch] = jnp.transpose(etab_ref[pl.ds(pl.multiple_of(blk * TILES, 8), TILES), :])
    bd[...] = jnp.zeros_like(bd)
    phacc[...] = jnp.zeros_like(phacc)

    def chunk(ch, _):
        blk = core * 16 + ch
        tt = jnp.concatenate([tab[32 * t + blk] for t in range(TILES)], axis=1).astype(bf16)
        etscr[...] = lax.dot_general(tt, spread, (((0,), (0,)), ((), ())), preferred_element_type=f32)

        def wtile(t, _):
            for pair in range(2):
                parts = []
                for kk in range(2):
                    k = 2 * pair + kk
                    ek = etscr[pl.ds(pl.multiple_of(t * 128 + PITCH * k, 8), NB), :]
                    p = pscr[pl.ds(ch * BLOCK + t * 4 + k, 1), :]
                    parts.append(jnp.concatenate([ek * p[:, 384 * a:384 * a + 384] for a in range(4)], axis=1))
                w = jnp.concatenate(parts, axis=0).astype(bf16)
                wscr[pl.ds(pl.multiple_of(t * 96 + pair * 48, 16), 48), :] = w
            return 0
        lax.fori_loop(0, TILES, wtile, 0, unroll=2)

        xscr[...] = jnp.dot(wscr[...], rt_ref[...], preferred_element_type=f32)

        ekt = ektscr[ch]

        for g in range(4):
            ep = []
            for h in range(2):
                evec = jnp.zeros((1, 128), f32)
                for k4 in range(4):
                    k = 8 * g + 4 * h + k4
                    p = kq_ref[ch * BLOCK + k]
                    pt = p // 4
                    pr = (pt % 32) * TILES + pt // 32
                    sh = (PITCH * (k4 + 4) - PITCH * (p % 4)) % 128
                    here = lane // PITCH == k4
                    e = pltpu.roll(tab[pt], sh, 1)
                    e = jnp.where(here, e, 0.0)
                    e = jnp.concatenate([e, jnp.zeros((8, 128), f32)], axis=0).astype(bf16)
                    bd[pl.ds(128 * h + PITCH * k4, PITCH), pl.ds(128 * h, 128)] = e
                    er = pltpu.roll(etab_ref[pl.ds(pr, 1), :], sh, 1)
                    evec = jnp.where(here, er, evec)
                ep.append(evec)
            for h in range(2):
                xs = [[None] * 4 for _ in range(2)]
                for k4 in range(4):
                    k = 8 * g + 4 * h + k4
                    for vt in range(2):
                        x = xscr[NB * k:NB * k + NB, 128 * vt:128 * vt + 128]
                        xs[vt][k4] = pltpu.roll(x, PITCH * k4, 1) if k4 else x
                for v in range(NV):
                    vt, s = VSLOT[v]
                    rel = (lane - NB * s + 128) % 128 // PITCH
                    y = xs[vt][3]
                    for k4 in range(3):
                        y = jnp.where(rel == k4, xs[vt][k4], y)
                    if s:
                        y = pltpu.roll(y, 128 - NB * s, 1)
                    ybuf[NB * v:NB * v + NB, 128 * h:128 * h + 128] = y
            z = jnp.dot(ybuf[...].astype(bf16), bd[...], preferred_element_type=f32)
            for h in range(2):
                t = 2 * g + h
                ek = jnp.zeros((NB, 128), f32)
                for k4 in range(4):
                    c = ekt[PITCH * k4:PITCH * k4 + NB, t:t + 1]
                    ek = jnp.where(lane // PITCH == k4, c, ek)
                diff = ep[h] - ek
                occ = jax.nn.sigmoid(ek * (-1.0 / KT)) - jax.nn.sigmoid(ep[h] * (-1.0 / KT))
                acc = jnp.zeros((NB, 128), f32)
                for v in range(NV):
                    zz = z[NB * v:NB * v + NB, 128 * h:128 * h + 128]
                    d = diff - freq_ref[v]
                    st = zz * zz * jnp.exp(d * d * (-1.0 / (2 * SIGMA * SIGMA)))
                    acc = acc + st
                    so = st * occ
                    phacc[v] += so[0:8] + so[8:16] + so[16:24]
                aescr[pl.ds(pl.multiple_of(ch * 4 * NB + NB * g, 8), NB), 128 * h:128 * h + 128] = acc
        return 0
    lax.fori_loop(0, 16, chunk, 0)
    sums = jnp.concatenate([jnp.sum(phacc[v], axis=0, keepdims=True) for v in range(NV)]
                           + [jnp.zeros((16 - NV, 128), f32)], axis=0)
    sums = jnp.sum(sums, axis=1, keepdims=True)
    phonon = jnp.where(lane == 96, sums[0:8], 0.0) + jnp.where(lane == 97, sums[8:16], 0.0)
    res = jnp.dot(aescr[...], fold, preferred_element_type=f32, precision=lax.Precision.HIGHEST)
    for ch in range(16):
        out = phonon
        for g in range(4):
            for t in range(3):
                a = 4 * NB * ch + NB * g + 8 * t
                piece = res[a:a + 8, :]
                sft = 32 * t + 8 * g
                out = out + (pltpu.roll(piece, sft, 1) if sft else piece)
        el_ref[ch] = out


def compute(core, kq, freq, phase, rt, eig, etab):
    f32, bf16 = jnp.float32, jnp.bfloat16
    smem = pl.BlockSpec(memory_space=pltpu.SMEM)
    vmem = pl.BlockSpec(memory_space=pltpu.VMEM)
    return pl.pallas_call(
        compute_kernel,
        out_shape=jax.ShapeDtypeStruct((16, 8, 128), f32),
        in_specs=[smem, smem, smem, vmem, vmem, vmem, vmem],
        out_specs=vmem,
        scratch_shapes=[
            pltpu.VMEM((256, NB, 128), f32),
            pltpu.VMEM((256, 128), f32),
            pltpu.VMEM((16 * BLOCK, NR * NB), f32),
            pltpu.VMEM((TILES * 128, 384), f32),
            pltpu.VMEM((16, 128, 8), f32),
            pltpu.VMEM((BLOCK * NB, NR * NB), bf16),
            pltpu.VMEM((BLOCK * NB, 256), f32),
            pltpu.VMEM((256, 256), bf16),
            pltpu.VMEM((NV * NB, 256), f32),
            pltpu.VMEM((64 * NB, 256), f32),
            pltpu.VMEM((NV, 8, 128), f32),
        ],
        compiler_params=pltpu.CompilerParams(vmem_limit_bytes=56 << 20),
        name="linewidths",
    )(core, kq, freq, phase, rt, eig, etab)


def place():
    ka, pb, row = lax.axis_index("ka"), lax.axis_index("pb"), lax.axis_index("row")
    return ka // 2, ka % 2, row, pb // 8, pb % 8


def device(y, core, x, y_lo, z):
    return {"ka": 2 * y + core, "pb": 8 * y_lo + z, "row": x}


def remote(src, dst, send, recv, target):
    return pltpu.make_async_remote_copy(src_ref=src, dst_ref=dst, send_sem=send, recv_sem=recv,
                                        device_id=target, device_id_type=pl.DeviceIdType.MESH)


def exchange_kernel(rs_ref, eg_ref, et_ref, rt_ref, eig_ref, etab_ref,
                    own, r_send, r_recv, t_send, t_recv, e_send, e_recv,
                    up_send, up_recv, dn_send, dn_recv,
                    rf_send, rf_recv, ef_send, ef_recv, tf_send, tf_recv):
    y, c, x, w, z = place()
    me = y * 4 + x
    partner = device(y, 1 - c, x, w, z)
    above = device(y, c, x, w, (z + 1) % 8)
    below = device(y, c, x, w, (z + 7) % 8)
    others = []
    for d in range(1, 16):
        yy, xx = (y + d // 4) % 4, (x + d % 4) % 4
        others.append((yy, xx, device(yy, c, xx, w, z)))

    barrier = pltpu.get_barrier_semaphore()
    for target in [o[2] for o in others] + [partner, above, below]:
        pl.semaphore_signal(barrier, inc=1, device_id=target, device_id_type=pl.DeviceIdType.MESH)
    pl.semaphore_wait(barrier, 18)

    copies = []
    locals_ = [
        pltpu.make_async_copy(eg_ref.at[z], eig_ref.at[z, c, me], own.at[0]),
        pltpu.make_async_copy(et_ref, etab_ref.at[c, me], own.at[1]),
        pltpu.make_async_copy(rs_ref.at[y, x], rt_ref.at[c, y, x], own.at[2]),
    ]
    for cp in locals_:
        cp.start()
    for n, (yy, xx, target) in enumerate(others):
        cp = remote(eg_ref.at[z], eig_ref.at[z, c, me], e_send.at[n], e_recv.at[n], target)
        cp.start()
        copies.append(cp)
    for n, (yy, xx, target) in enumerate(others):
        cp = remote(et_ref, etab_ref.at[c, me], t_send.at[n], t_recv.at[n], target)
        cp.start()
        copies.append(cp)
    for n, (yy, xx, target) in enumerate(others):
        cp = remote(rs_ref.at[yy, xx], rt_ref.at[c, y, x], r_send.at[n], r_recv.at[n], target)
        cp.start()
        copies.append(cp)

    def arrival(ref, recv):
        pltpu.make_async_copy(ref, ref, recv).wait()

    locals_[0].wait()
    for n in range(15):
        yy, xx = (y + 16 - (n + 1) // 4) % 4, (x + 16 - (n + 1) % 4) % 4
        arrival(eig_ref.at[z, c, yy * 4 + xx], e_recv.at[n])
    for step in range(4):
        for part in range(4):
            if step:
                arrival(eig_ref.at[(z + 8 - step) % 8, c, pl.ds(4 * part, 4)], up_recv.at[step - 1, part])
            src = eig_ref.at[(z + 8 - step) % 8, c, pl.ds(4 * part, 4)]
            cp = remote(src, src, up_send.at[step, part], up_recv.at[step, part], above)
            cp.start()
            copies.append(cp)
            if step < 3 or step == 3:
                if step:
                    arrival(eig_ref.at[(z + step) % 8, c, pl.ds(4 * part, 4)], dn_recv.at[step - 1, part])
                if step < 3:
                    src = eig_ref.at[(z + step) % 8, c, pl.ds(4 * part, 4)]
                    cp = remote(src, src, dn_send.at[step, part], dn_recv.at[step, part], below)
                    cp.start()
                    copies.append(cp)
        done = [(z + 8 - step) % 8] if step == 0 else [(z + 8 - step) % 8, (z + step) % 8]
        for m, t in enumerate(done):
            f = step if m == 0 else 4 + step
            cp = remote(eig_ref.at[t, c], eig_ref.at[t, c], ef_send.at[f], ef_recv.at[f], partner)
            cp.start()
            copies.append(cp)
    locals_[1].wait()
    for n in range(15):
        yy, xx = (y + 16 - (n + 1) // 4) % 4, (x + 16 - (n + 1) % 4) % 4
        arrival(etab_ref.at[c, yy * 4 + xx], t_recv.at[n])
    cp = remote(etab_ref.at[c], etab_ref.at[c], tf_send.at[0], tf_recv.at[0], partner)
    cp.start()
    copies.append(cp)
    locals_[2].wait()
    for dy in range(4):
        yy = (y + 4 - dy) % 4
        for dx in range(4):
            n = 4 * dy + dx - 1
            if n >= 0:
                arrival(rt_ref.at[c, yy, (x + 4 - dx) % 4], r_recv.at[n])
        cp = remote(rt_ref.at[c, yy], rt_ref.at[c, yy], rf_send.at[dy], rf_recv.at[dy], partner)
        cp.start()
        copies.append(cp)
    for part in range(4):
        arrival(eig_ref.at[(z + 4) % 8, c, pl.ds(4 * part, 4)], up_recv.at[3, part])
    cp = remote(eig_ref.at[(z + 4) % 8, c], eig_ref.at[(z + 4) % 8, c], ef_send.at[4], ef_recv.at[4], partner)
    cp.start()
    copies.append(cp)
    for f in range(8):
        t = (z + 8 - f) % 8 if f < 5 else (z + f - 4) % 8
        arrival(eig_ref.at[t, 1 - c], ef_recv.at[f])
    arrival(etab_ref.at[1 - c], tf_recv.at[0])
    for dy in range(4):
        arrival(rt_ref.at[1 - c, (y + 4 - dy) % 4], rf_recv.at[dy])
    for cp in copies:
        cp.wait_send()


def exchange(rs, eg, et):
    vmem = pl.BlockSpec(memory_space=pltpu.VMEM)
    dma = pltpu.SemaphoreType.DMA
    return pl.pallas_call(
        exchange_kernel,
        out_shape=(jax.ShapeDtypeStruct((2, 4, 4, 48, 256), jnp.bfloat16),
                   jax.ShapeDtypeStruct((8, 2, 16, NB, 128), jnp.bfloat16),
                   jax.ShapeDtypeStruct((2, 16, 8, 128), jnp.float32)),
        in_specs=[vmem] * 3,
        out_specs=(vmem,) * 3,
        scratch_shapes=[dma((3,)), dma((15,)), dma((15,)), dma((15,)), dma((15,)), dma((15,)), dma((15,)),
                        dma((4, 4)), dma((4, 4)), dma((3, 4)), dma((3, 4)),
                        dma((4,)), dma((4,)), dma((8,)), dma((8,)), dma((1,)), dma((1,))],
        compiler_params=pltpu.CompilerParams(collective_id=0, has_side_effects=True),
        name="exchange",
    )(rs, eg, et)


def reduce_kernel(el_ref, out_ref, got, mine, peers, half, own, a_send, a_recv, b_send, b_recv, p_send, p_recv):
    f32 = jnp.float32
    y, c, x, w, z = place()
    me = y * 4 + x
    partner = device(y, 1 - c, x, w, z)
    plane, column = [], []
    for d in range(1, 16):
        yy, xx = (y + d // 4) % 4, (x + d % 4) % 4
        plane.append((yy * 4 + xx, device(yy, c, xx, w, z)))
        ww, zz = (w + d // 8) % 2, (z + d % 8) % 8
        column.append((ww * 8 + zz, device(y, c, x, ww, zz)))
    barrier = pltpu.get_barrier_semaphore()
    for target in [o[1] for o in plane + column] + [partner]:
        pl.semaphore_signal(barrier, inc=1, device_id=target, device_id_type=pl.DeviceIdType.MESH)
    pl.semaphore_wait(barrier, 31)

    copies = []
    for n, (block, target) in enumerate(plane):
        cp = remote(el_ref.at[block], got.at[me], a_send.at[n], a_recv.at[n], target)
        cp.start()
        copies.append(cp)
    cp = pltpu.make_async_copy(el_ref.at[me], got.at[me], own.at[0])
    cp.start()
    cp.wait()
    for n in range(15):
        yy, xx = (y + 16 - (n + 1) // 4) % 4, (x + 16 - (n + 1) % 4) % 4
        ref = got.at[yy * 4 + xx]
        pltpu.make_async_copy(ref, ref, a_recv.at[n]).wait()
    lane = lax.broadcasted_iota(jnp.int32, (8, 128), 1)
    total = jnp.zeros((8, 128), f32)
    phonon = jnp.zeros((8, 128), f32)
    for s in range(16):
        tile = got[s]
        total = total + tile
        phonon = phonon + pltpu.roll(jnp.where((lane == 96) | (lane == 97), tile, 0.0), (2 * s + 32) % 128, 1)
    mine[...] = total
    half[0] = phonon
    for n, (block, target) in enumerate(column):
        cp = remote(mine, peers.at[w * 8 + z], b_send.at[n], b_recv.at[n], target)
        cp.start()
        copies.append(cp)
    cp = remote(half.at[0], half.at[1], p_send.at[0], p_recv.at[0], partner)
    cp.start()
    copies.append(cp)
    for n in range(15):
        ww, zz = (w + 2 - (n + 1) // 8) % 2, (z + 16 - (n + 1) % 8) % 8
        ref = peers.at[ww * 8 + zz]
        pltpu.make_async_copy(ref, ref, b_recv.at[n]).wait()
    pltpu.make_async_copy(half.at[1], half.at[1], p_recv.at[0]).wait()
    acc = jnp.zeros((8, 128), f32)
    for s in range(16):
        acc = acc + jnp.where(s == w * 8 + z, total, peers[s])
    out_ref[0] = acc
    out_ref[1] = half[0] + half[1]
    for cp in copies:
        cp.wait_send()


def reduce(el):
    f32 = jnp.float32
    vmem = pl.BlockSpec(memory_space=pltpu.VMEM)
    dma = pltpu.SemaphoreType.DMA
    return pl.pallas_call(
        reduce_kernel,
        out_shape=jax.ShapeDtypeStruct((2, 8, 128), f32),
        in_specs=[vmem],
        out_specs=vmem,
        scratch_shapes=[pltpu.VMEM((16, 8, 128), f32), pltpu.VMEM((8, 128), f32), pltpu.VMEM((16, 8, 128), f32),
                        pltpu.VMEM((2, 8, 128), f32),
                        dma((1,)), dma((15,)), dma((15,)), dma((15,)), dma((15,)), dma((1,)), dma((1,))],
        compiler_params=pltpu.CompilerParams(collective_id=1, has_side_effects=True),
        name="reduce",
    )(el)


def phase_table(lattice, kpoint_rows):
    rvec = lattice.astype(jnp.float32)
    argument = (
        rvec[:, 0:1] * kpoint_rows[:, 0][None, :]
        + rvec[:, 1:2] * kpoint_rows[:, 1][None, :]
        + rvec[:, 2:3] * kpoint_rows[:, 2][None, :]
    )
    return jnp.cos(2.0 * math.pi * argument).astype(jnp.bfloat16)


def on_device(coupling, rotation, freq, eigvec, energies, window, kq_index, kpoints, lattice):
    f32, bf16 = jnp.float32, jnp.bfloat16
    y, c, x, w, z = place()
    coup = coupling.reshape(4, 2, NM, NB, NB)
    rotated = jnp.einsum("qrcij,qcv->qrvij", coup, rotation, preferred_element_type=f32).astype(bf16)
    rs = rotated.reshape(4, 2, 4, NV, NB, NB).transpose(0, 2, 1, 5, 3, 4).reshape(4, 4, 48, NV, NB)
    low = jnp.pad(rs[:, :, :, :5].reshape(4, 4, 48, 120), ((0, 0), (0, 0), (0, 0), (0, 8)))
    high = jnp.pad(rs[:, :, :, 5:].reshape(4, 4, 48, 96), ((0, 0), (0, 0), (0, 0), (0, 32)))
    rs = jnp.concatenate([low, high], axis=-1)
    eg = jnp.pad(eigvec.reshape(8, 4, NB, NB), ((0, 0), (0, 0), (0, 0), (0, 8)))
    eg = eg.transpose(0, 2, 1, 3).reshape(8, NB, 128)
    et = jnp.concatenate([energies, window.astype(f32)[:, None], jnp.zeros((32, 7), f32)], axis=1).reshape(8, 128)
    rt, eig, etab = exchange(rs, eg, et)

    lat = lattice.reshape(4, 2, 4, 2, 3).transpose(1, 0, 2, 3, 4).reshape(NR, 3)
    kp = lax.dynamic_index_in_dim(kpoints.reshape(4, 2, 128, 3), c, 1, keepdims=False).reshape(512, 3)
    phase = phase_table(lat, kp).T
    kq = lax.dynamic_index_in_dim(kq_index.reshape(4, 4, 2, 128), y, 0, keepdims=False)
    kq = lax.dynamic_index_in_dim(kq, c, 1, keepdims=False).reshape(512)
    slot = ((kq // 4) % 8) * 32 + ((kq // 128) % 2) * 16 + (kq // 256) * 4 + (kq // 32) % 4
    kq = slot * 4 + kq % 4
    fr = lax.dynamic_slice(freq, (y, NV * x), (1, NV)).reshape(NV)
    el = compute(c.reshape(1).astype(jnp.int32), kq, fr, phase, rt.reshape(NR * NB, 256),
                 eig.reshape(256, NB, 128), etab.reshape(256, 128))
    out = reduce(el)
    norm = 1.0 / (math.sqrt(2.0 * math.pi) * SIGMA)
    electron = out[0, :, :96].reshape(8, 3, 32).transpose(2, 1, 0).reshape(32, NB) * (norm / 55296.0)
    phonon = out[1, :, :32].reshape(8, 16, 2).transpose(1, 2, 0).reshape(16, 16)[:, :NV].reshape(4, NM) * (norm / 24576.0)
    return electron, phonon


def solution(mesh):
    return jax.shard_map(
        on_device,
        mesh=mesh,
        in_specs=(
            P("pb", ("ka", "row"), None),
            P("pb", None, None),
            P("pb", None),
            P(("ka", "row"), None, None),
            P(("ka", "row"), None),
            P(("ka", "row")),
            P("pb", None),
            P(),
            P(),
        ),
        out_specs=(P(("ka", "row"), None), P("pb", None)),
        check_vma=False,
    )
```

time: 555 us -> 131 us (0.24); the launches traced: 544 us -> 130 us
  blocking collectives: 353 us -> 0 us
  Pallas kernels: 0 us -> 108 us
  matrix products: 101 us -> 0.44 us
  local copies, waits for them, and re-layouts: 63.2 us -> 16 us
  between operations: 14.9 us -> 0.87 us
  waiting for transfers between devices: 8.77 us -> 0 us
    psum x2 -> x0, blocking collectives: 200 us -> none  [the longest x1 149 us: on_device(): phonon = lax.psum(phon_local, ('ka', 'row'))]
    pallas_call x0 -> x3, Pallas kernels: none -> 108 us  [the longest x1 47.3 us: compute(): pl.pallas_call(compute_kernel, out_shape=jax.ShapeDtypeStruct((16, 8, 128...]
    dot_general x3 -> x0, matrix products: 101 us -> none  [the longest x1 69.3 us: block_terms(): jnp.einsum('imc,binc->bmnc', eig_kq, right, preferred_element_type=jnp.fl...]
    all_gather x1 -> x0, blocking collectives: 79.1 us -> none  [on_device(): lax.all_gather(energies, ('ka', 'row'), axis=0, tiled=True)]
    unnamed x1 -> x0, blocking collectives: 73.2 us -> none
    reshape x3 -> x10, local copies, waits for them, and re-layouts: 47.4 us -> 9.65 us  [the longest x2 4.86 us: on_device(): coup = coupling.reshape(4, 2, NM, NB, NB)]
    all_gather x2 -> x0, waiting for transfers between devices: 8.73 us -> none  [the longest x1 8.73 us: on_device(): coup_full = lax.all_gather(coupling, ('ka', 'row'), axis=1, tiled=True)]
    unnamed x14 -> x12, local copies, waits for them, and re-layouts: 7.06 us -> 0.21 us
  transfers between devices with their start and end apart: 2 -> 0, of which waited for: 1 -> 0; matrix products, arithmetic and copies ran while one was open for 3% -> 0% of each run, Pallas kernels for 0% -> 0%
where the time goes in v1:
time: 131 us; the launch traced here: 130 us
  Pallas kernels  108 us (82%)
  local copies, waits for them, and re-layouts  16 us (12%)
  other arithmetic  4.69 us (4%)
    pallas_call x1, Pallas kernels, compute(): pl.pallas_call(compute_kernel, out_shape=jax.ShapeDtypeStruct((16, 8, 128...  47.3 us
    pallas_call x1, Pallas kernels, exchange(): pl.pallas_call(exchange_kernel, out_shape=(jax.ShapeDtypeStruct((2, 4, 4,...  42.2 us
    pallas_call x1, Pallas kernels, reduce(): pl.pallas_call(reduce_kernel, out_shape=jax.ShapeDtypeStruct((2, 8, 128),...  18.5 us
    reshape x2, local copies, waits for them, and re-layouts, on_device(): coup = coupling.reshape(4, 2, NM, NB, NB)  4.86 us

profile of v1, /device:TPU:1, one launch (start us, length us, event | category | flops | bytes accessed | tf_op | source)
XLA Modules:
  0.0 130.1 jit_solution(12031035661946669730)
XLA Ops:
  0.7 0.7 reshape.81
  1.5 0.7 convert_element_type.31
  2.2 0.1 convert_element_type.32
  2.3 0.1 convert_element_type.34
  2.4 1.6 %cosine_convert_fusion.phase_ref = bf16[512,64]{1,0:T(8,128)(2,1)} fusion(f32[64]{0:T(128)S(1)} %get-tuple-element.13, f32[512]{0:T(512)S(1)} %bitcast.73, f32[64]{0:T(128)S(1)} %get-tuple-element.12, f32[512]{0:T(512)S(1)} %bitcast.74, f32[64]{0:T(128)S(1)} %get-tuple-element.11, f32[512]{0:T(512)S(1)} %bitcast.72), kind=kLoop, calls=%fused_computation.6 | loop fusion | flops 229376 | bytes 72448 | tf_op jit(solution)/shard_map/convert_element_type | solution.py:390
  4.1 0.7 dynamic-slice_bitcast_fusion.freq_ref
  4.7 0.7 reshape.78
  5.5 0.6 fusion.11.kq_ref
  6.1 3.4 %reshape.83 = bf16[4,2,36,24,24]{4,3,2,1,0:T(8,128)(2,1)S(1)} reshape(bf16[4,2,20736]{2,1,0:T(2,128)(2,1)} %param.9) | data formatting | bytes 663552 | tf_op jit(solution)/shard_map/reshape | solution.py:396
  9.5 1.5 %copy.46 = bf16[4,2,36,24,24]{2,4,3,1,0:T(8,128)(2,1)S(1)} copy(bf16[4,2,36,24,24]{4,3,2,1,0:T(8,128)(2,1)S(1)} %reshape.83) | data formatting | bytes 663552 | tf_op jit(solution)/shard_map/reshape | solution.py:396
  11.0 0.4 fusion.3
  11.4 0.2 convert_bitcast_fusion
  11.6 1.7 %copy.47 = bf16[4,2,36,24,24]{4,3,2,1,0:T(8,128)(2,1)S(1)} copy(bf16[4,2,36,24,24]{2,4,3,1,0:T(8,128)(2,1)S(1)} %convert_bitcast_fusion) | data formatting | bytes 663552 | tf_op jit(solution)/shard_map/convert_element_type | solution.py:397
  13.3 1.6 %copy.48 = bf16[4,4,2,24,9,24]{3,2,5,4,1,0:T(2,128)(2,1)S(1)} copy(bf16[4,4,2,24,9,24]{3,5,4,1,2,0:T(8,128)(2,1)S(1)} %bitcast.57) | data formatting | bytes 663552 | tf_op jit(solution)/shard_map/transpose | solution.py:398
  14.9 0.8 reshape.85
  15.8 0.2 copy.49
  16.1 0.2 copy.50
  16.2 0.8 fusion.2.rs_ref
  17.1 0.2 copy.51
  17.3 0.1 copy.52
  17.4 0.8 reshape.89.eg_ref
  18.4 0.7 reshape.90.et_ref
  19.1 42.2 %exchange.1 = (bf16[2,4,4,48,256]{4,3,2,1,0:T(8,128)(2,1)}, bf16[8,2,16,24,128]{4,3,2,1,0:T(8,128)(2,1)}, f32[2,16,8,128]{3,2,1,0:T(8,128)}) custom-call(bf16[4,4,48,256]{3,2,1,0:T(8,128)(2,1)} %fusion.2.rs_ref, bf16[8,24,128]{2,1,0:T(8,128)(2,1)} %reshape.89.eg_ref, f32[8,128]{1,0:T(8,128)} %reshape.90.et_ref), custom_call_target="tpu_custom_call" | custom-call | tf_op jit(solution)/shard_map/exchange/pallas_call | solution.py:293
  61.3 47.3 %linewidths.1.el_ref = f32[16,8,128]{2,1,0:T(8,128)} custom-call(s32[1]{0:T(128)} %bitcast.core_ref, s32[512]{0:T(512)} %fusion.11.kq_ref, f32[9]{0:T(128)} %dynamic-slice_bitcast_fusion.freq_ref, bf16[512,64]{1,0:T(8,128)(2,1)} %cosine_convert_fusion.phase_ref, bf16[1536,256]{1,0:T(8,128)(2,1)} %bitcast.63, bf16[256,24,128]{2,1,0:T(8,128)(2,1)} %bitcast.61, ...), custom_call_target="tpu_custom_call" | custom-call | tf_op jit(solution)/shard_map/linewidths/pallas_call | solution.py:152
  108.6 18.5 %reduce.5 = f32[2,8,128]{2,1,0:T(8,128)} custom-call(f32[16,8,128]{2,1,0:T(8,128)} %linewidths.1.el_ref), custom_call_target="tpu_custom_call" | custom-call | tf_op jit(solution)/shard_map/reduce/pallas_call | solution.py:370
  127.1 0.7 slice.42
  127.8 0.1 copy.55
  128.0 0.1 copy.57
  128.1 0.7 mul.133
  128.7 0.7 slice_multiply_fusion.1
  129.4 0.1 mul.128
  129.5 0.6 copy.63
  (26 shorter events, 0.6 us)
Async XLA Ops:
  0.6 3.4 %copy-start = (f32[4,36]{1,0:T(4,128)S(1)}, f32[4,36]{1,0:T(4,128)}, u32[]{:S(2)}) copy-start(f32[4,36]{1,0:T(4,128)} %param.11) | copy-start | bytes 1732
  9.4 1.5 %copy-start.2 = (bf16[4,36,36]{2,0,1:T(4,128)(2,1)S(1)}, bf16[4,36,36]{2,0,1:T(4,128)(2,1)}, u32[]{:S(2)}) copy-start(bf16[4,36,36]{2,0,1:T(4,128)(2,1)} %param.10) | copy-start | bytes 31108
  15.8 1.3 %copy-start.1 = (bf16[32,24,24]{0,2,1:T(8,128)(2,1)S(1)}, bf16[32,24,24]{0,2,1:T(8,128)(2,1)}, u32[]{:S(2)}) copy-start(bf16[32,24,24]{0,2,1:T(8,128)(2,1)} %param.12) | copy-start | bytes 110596
  16.0 2.2 %copy-start.4 = (s32[32]{0:T(128)S(1)}, s32[32]{0:T(128)}, u32[]{:S(2)}) copy-start(s32[32]{0:T(128)} %param.14) | copy-start | bytes 388
  16.1 2.2 %copy-start.3 = (f32[32,24]{0,1:T(8,128)S(1)}, f32[32,24]{0,1:T(8,128)}, u32[]{:S(2)}) copy-start(f32[32,24]{0,1:T(8,128)} %param.13) | copy-start | bytes 9220

commit v2 on v0

v2 whole, which is shorter than its diff:
```python
import math

import jax
import jax.numpy as jnp
from jax import lax
from jax.experimental import pallas as pl
from jax.experimental.pallas import tpu as pltpu
from jax.sharding import PartitionSpec as P

SIGMA = 0.1
KT = 0.2
NB, NM, NR = 24, 36, 64
NV = 9
PITCH = 32
VSLOT = [(v // 5, v % 5) for v in range(NV)]


def constants():
    f32, bf16 = jnp.float32, jnp.bfloat16
    r1 = lax.broadcasted_iota(jnp.int32, (NB, 384), 0)
    c1 = lax.broadcasted_iota(jnp.int32, (NB, 384), 1)
    spread = jnp.where(c1 % NB == r1, 1.0, 0.0).astype(bf16)
    r2 = lax.broadcasted_iota(jnp.int32, (NR, NR * NB), 0)
    c2 = lax.broadcasted_iota(jnp.int32, (NR, NR * NB), 1)
    widen = jnp.where(c2 // NB == r2, 1.0, 0.0).astype(bf16)
    return spread, widen


def right_stage(t, c, rt_ref, eig_ref, spread, pscr, etscr, wbufs, xscr):
    f32, bf16 = jnp.float32, jnp.bfloat16
    tt = jnp.concatenate([eig_ref[32 * t + 16 * c + b] for b in range(16)], axis=1)
    etscr[...] = lax.dot_general(tt, spread, (((0,), (0,)), ((), ())), preferred_element_type=f32)
    for sub in range(4):
        wbuf = wbufs[sub % 2]
        for pair in range(8):
            parts = []
            for kk in range(2):
                k = 16 * sub + 2 * pair + kk
                ek = etscr[PITCH * k:PITCH * k + NB, :]
                p = pscr[pl.ds((k // 4) * 32 + 4 * t + k % 4, 1), :]
                parts.append(jnp.concatenate([ek * p[:, 384 * a:384 * a + 384] for a in range(4)], axis=1))
            wbuf[48 * pair:48 * pair + 48, :] = jnp.concatenate(parts, axis=0).astype(bf16)
        xscr[t, 384 * sub:384 * sub + 384, :] = jnp.dot(wbuf[...], rt_ref[...].reshape(NR * NB, 256), preferred_element_type=f32)


def final_stage(t, c, q, vq, kq_ref, freq_ref, eig_ref, etab_ref, xscr, bds, ybufs, aes, phacc, acc_ref):
    f32, bf16 = jnp.float32, jnp.bfloat16
    lane = lax.broadcasted_iota(jnp.int32, (1, 128), 1)
    ekt = jnp.transpose(etab_ref[pl.ds(pl.multiple_of(32 * t + 16 * c, 16), 16), :])
    for g in range(8):
        bd, ybuf = bds.at[g % 4], ybufs.at[g % 4]
        eps = []
        for h in range(2):
            b = 2 * g + h
            evec = jnp.zeros((1, 128), f32)
            for k4 in range(4):
                p = kq_ref[q, 4 * t + c * 128 + (b // 4) * 256 + (b % 4) * 32 + k4]
                tile = ((p >> 2) & 7) * 32 + ((p >> 7) & 1) * 16 + ((p >> 8) << 2) + ((p >> 5) & 3)
                sh = ((k4 - p) & 3) * PITCH
                here = lane // PITCH == k4
                e = pltpu.roll(eig_ref[tile].astype(f32), sh, 1)
                e = jnp.where(here, e, 0.0)
                e = jnp.concatenate([e, jnp.zeros((8, 128), f32)], axis=0).astype(bf16)
                bd[128 * h + PITCH * k4:128 * h + PITCH * k4 + PITCH, 128 * h:128 * h + 128] = e
                er = pltpu.roll(etab_ref[pl.ds(tile, 1), :], sh, 1)
                evec = jnp.where(here, er, evec)
            eps.append(evec)
        for h in range(2):
            xs = [[None] * 4 for _ in range(2)]
            for k4 in range(4):
                k = 8 * g + 4 * h + k4
                for vt in range(2):
                    x = xscr[t, NB * k:NB * k + NB, 128 * vt:128 * vt + 128]
                    xs[vt][k4] = pltpu.roll(x, PITCH * k4, 1) if k4 else x
            for v in range(NV):
                vt, s = VSLOT[v]
                rel = (lane - NB * s + 128) % 128 // PITCH
                yv = xs[vt][3]
                for k4 in range(3):
                    yv = jnp.where(rel == k4, xs[vt][k4], yv)
                if s:
                    yv = pltpu.roll(yv, 128 - NB * s, 1)
                ybuf[NB * v:NB * v + NB, 128 * h:128 * h + 128] = yv
        zz = jnp.dot(ybuf[...].astype(bf16), bd[...], preferred_element_type=f32)
        for h in range(2):
            b = 2 * g + h
            ek = jnp.zeros((NB, 128), f32)
            for k4 in range(4):
                ek = jnp.where(lane // PITCH == k4, ekt[PITCH * k4:PITCH * k4 + NB, b:b + 1], ek)
            diff = eps[h] - ek
            occ = jax.nn.sigmoid(ek * (-1.0 / KT)) - jax.nn.sigmoid(eps[h] * (-1.0 / KT))
            acc = jnp.zeros((NB, 128), f32)
            for v in range(NV):
                zv = zz[NB * v:NB * v + NB, 128 * h:128 * h + 128]
                d = diff - freq_ref[q, NV * vq + v]
                st = zv * zv * jnp.exp(d * d * (-1.0 / (2 * SIGMA * SIGMA)))
                acc = acc + st
                so = st * occ
                phacc[v] += so[0:8] + so[8:16] + so[16:24]
            aes[NB * g:NB * g + NB, 128 * h:128 * h + 128] = acc
    r3 = lax.broadcasted_iota(jnp.int32, (256, 128), 0)
    c3 = lax.broadcasted_iota(jnp.int32, (256, 128), 1)
    fold = jnp.where(c3 == (r3 // 128) * 64 + 4 * t + (r3 % 128) // PITCH, 1.0, 0.0).astype(f32)
    acc_ref[...] += jnp.dot(aes[...], fold, preferred_element_type=f32, precision=lax.Precision.HIGHEST)


def pack_sums(phacc, acc_ref, el_ref):
    f32 = jnp.float32
    lane = lax.broadcasted_iota(jnp.int32, (1, 128), 1)
    sums = jnp.concatenate([jnp.sum(phacc[v], axis=0, keepdims=True) for v in range(NV)]
                           + [jnp.zeros((16 - NV, 128), f32)], axis=0)
    sums = jnp.sum(sums, axis=1, keepdims=True)
    phonon = jnp.where(lane == 96, sums[0:8], 0.0) + jnp.where(lane == 97, sums[8:16], 0.0)
    for b in range(16):
        out = phonon
        for u in range(3):
            a = NB * (b // 2) + 8 * u
            piece = jnp.where(lane // 64 == b % 2, acc_ref[a:a + 8, :], 0.0)
            shift = (32 * u + 64 * (b % 2)) % 128
            out = out + (pltpu.roll(piece, shift, 1) if shift else piece)
        el_ref[b] = out


def place():
    ka, pb, row = lax.axis_index("ka"), lax.axis_index("pb"), lax.axis_index("row")
    return ka // 2, ka % 2, row, pb // 8, pb % 8


def device(y, core, x, y_lo, z):
    return {"ka": 2 * y + core, "pb": 8 * y_lo + z, "row": x}


def phases(y_unused, c, kp_ref, lat_ref, widen, pscr):
    f32 = jnp.float32
    lat = lat_ref[...].astype(f32)
    for u in range(4):
        cols = pl.ds(pl.multiple_of(256 * u + 128 * c, 128), 128)
        arg = (lat[:, 0:1] * kp_ref[0:1, cols] + lat[:, 1:2] * kp_ref[1:2, cols]
               + lat[:, 2:3] * kp_ref[2:3, cols])
        ph = jnp.cos(2.0 * math.pi * arg).astype(jnp.bfloat16)
        pscr[128 * u:128 * u + 128, :] = lax.dot_general(
            ph, widen, (((0,), (0,)), ((), ())), preferred_element_type=f32)


def mega_kernel(kq_ref, freq_ref, kp_ref, lat_ref, rs_ref, eg_ref, et_ref, out_ref,
                rt, eig, etab, pscr, etscr, wa, wb, xscr, bds, ybufs, aes, phacc, acc_ref,
                el, got, mine, peers, half,
                own, r_send, r_recv, t_send, t_recv, e_send, e_recv,
                up_send, up_recv, dn_send, dn_recv, ut_send, ut_recv, dt_send, dt_recv,
                rf_send, rf_recv, ef_send, ef_recv, tf_send, tf_recv,
                a_send, a_recv, b_send, b_recv, p_send, p_recv):
    f32 = jnp.float32
    y, c, x, w, z = place()
    me = y * 4 + x
    partner = device(y, 1 - c, x, w, z)
    above = device(y, c, x, w, (z + 1) % 8)
    below = device(y, c, x, w, (z + 7) % 8)
    plane, column = [], []
    for d in range(1, 16):
        yy, xx = (y + d // 4) % 4, (x + d % 4) % 4
        plane.append((yy, xx, device(yy, c, xx, w, z)))
        ww, zz = (w + d // 8) % 2, (z + d % 8) % 8
        column.append(device(y, c, x, ww, zz))

    barrier = pltpu.get_barrier_semaphore()
    for target in [o[2] for o in plane] + column + [partner]:
        pl.semaphore_signal(barrier, inc=1, device_id=target, device_id_type=pl.DeviceIdType.MESH)

    local = [
        pltpu.make_async_copy(eg_ref.at[z], eig.at[32 * z + 16 * c + me], own.at[0]),
        pltpu.make_async_copy(et_ref.at[pl.ds(z, 1)], etab.at[pl.ds(32 * z + 16 * c + me, 1)], own.at[1]),
        pltpu.make_async_copy(rs_ref.at[y, x], rt.at[y, c, x], own.at[2]),
    ]
    for cp in local:
        cp.start()
    pl.semaphore_wait(barrier, 31)

    copies = []

    def send(src, dst, s, r, target):
        cp = pltpu.make_async_remote_copy(src_ref=src, dst_ref=dst, send_sem=s, recv_sem=r, device_id=target,
                                          device_id_type=pl.DeviceIdType.MESH)
        cp.start()
        return cp

    def arrival(ref, recv):
        pltpu.make_async_copy(ref, ref, recv).wait()

    def tiles(t, core):
        return eig.at[pl.ds(32 * t + 16 * core, 16)]

    def rows(t, core):
        return etab.at[pl.ds(pl.multiple_of(32 * t + 16 * core, 16), 16)]

    here = 32 * z + 16 * c + me
    for n, (yy, xx, target) in enumerate(plane):
        copies.append(send(eg_ref.at[z], eig.at[here], e_send.at[n], e_recv.at[n], target))
        copies.append(send(et_ref.at[pl.ds(z, 1)], etab.at[pl.ds(here, 1)], t_send.at[n], t_recv.at[n], target))
    for n, (yy, xx, target) in enumerate(plane):
        copies.append(send(rs_ref.at[yy, xx], rt.at[y, c, x], r_send.at[n], r_recv.at[n], target))

    spread, widen = constants()
    phases(y, c, kp_ref, lat_ref, widen, pscr)
    bds[...] = jnp.zeros_like(bds)
    phacc[...] = jnp.zeros_like(phacc)
    acc_ref[...] = jnp.zeros_like(acc_ref)

    def ring(step):
        up, dn = (z + 8 - step) % 8, (z + step) % 8
        if step:
            arrival(tiles(up, c), up_recv.at[step - 1])
            arrival(rows(up, c), ut_recv.at[step - 1])
        if step < 4:
            send(tiles(up, c), tiles(up, c), up_send.at[step], up_recv.at[step], above)
            send(rows(up, c), rows(up, c), ut_send.at[step], ut_recv.at[step], above)
        if 0 < step < 4:
            arrival(tiles(dn, c), dn_recv.at[step - 1])
            arrival(rows(dn, c), dt_recv.at[step - 1])
        if step < 3:
            send(tiles(dn, c), tiles(dn, c), dn_send.at[step], dn_recv.at[step], below)
            send(rows(dn, c), rows(dn, c), dt_send.at[step], dt_recv.at[step], below)
        for f, t in [(step, up)] + ([(4 + step, dn)] if 0 < step < 4 else []):
            send(tiles(t, c), tiles(t, c), ef_send.at[f], ef_recv.at[f], partner)
            send(rows(t, c), rows(t, c), tf_send.at[f], tf_recv.at[f], partner)

    def slice_of(f):
        return (z + 8 - f) % 8 if f < 5 else (z + f - 4) % 8

    for cp in local:
        cp.wait()
    for n in range(15):
        d = n + 1
        b = (y + 4 - d // 4) % 4 * 4 + (x + 4 - d % 4) % 4
        arrival(eig.at[32 * z + 16 * c + b], e_recv.at[n])
        arrival(etab.at[pl.ds(32 * z + 16 * c + b, 1)], t_recv.at[n])
    ring(0)
    ring(1)
    for dy in range(4):
        yy = (y + 4 - dy) % 4
        for dx in range(4):
            if dy or dx:
                arrival(rt.at[yy, c, (x + 4 - dx) % 4], r_recv.at[4 * dy + dx - 1])
        copies.append(send(rt.at[yy, c], rt.at[yy, c], rf_send.at[dy], rf_recv.at[dy], partner))
    for dy in range(4):
        arrival(rt.at[(y + 4 - dy) % 4, 1 - c], rf_recv.at[dy])

    def right(i, _):
        for step, at in ((2, 1), (3, 3), (4, 5)):
            pl.when(i == at)(lambda step=step: ring(step))
        t = (z + 8 + (1 - 2 * (i % 2)) * ((i + 1) // 2)) % 8
        right_stage(t, c, rt, eig, spread, pscr, etscr, (wa, wb), xscr)
        return 0
    lax.fori_loop(0, 8, right, 0)

    for f in range(8):
        arrival(tiles(slice_of(f), 1 - c), ef_recv.at[f])
        arrival(rows(slice_of(f), 1 - c), tf_recv.at[f])

    def final(t, _):
        final_stage(t, c, y, x, kq_ref, freq_ref, eig, etab, xscr, bds, ybufs, aes, phacc, acc_ref)
        return 0
    lax.fori_loop(0, 8, final, 0)
    pack_sums(phacc, acc_ref, el)

    for n, (yy, xx, target) in enumerate(plane):
        copies.append(send(el.at[yy * 4 + xx], got.at[me], a_send.at[n], a_recv.at[n], target))
    for n in range(15):
        d = n + 1
        arrival(got.at[(y + 4 - d // 4) % 4 * 4 + (x + 4 - d % 4) % 4], a_recv.at[n])
    lane = lax.broadcasted_iota(jnp.int32, (8, 128), 1)
    total = jnp.zeros((8, 128), f32)
    phonon = jnp.zeros((8, 128), f32)
    for s in range(16):
        tile = jnp.where(me == s, el[s], got[s])
        total = total + tile
        phonon = phonon + pltpu.roll(jnp.where((lane == 96) | (lane == 97), tile, 0.0), (2 * s + 32) % 128, 1)
    mine[...] = total
    half[0] = phonon
    for n, target in enumerate(column):
        copies.append(send(mine, peers.at[w * 8 + z], b_send.at[n], b_recv.at[n], target))
    copies.append(send(half.at[0], half.at[1], p_send.at[0], p_recv.at[0], partner))
    for n in range(15):
        d = n + 1
        arrival(peers.at[(w + 2 - d // 8) % 2 * 8 + (z + 8 - d % 8) % 8], b_recv.at[n])
    arrival(half.at[1], p_recv.at[0])
    acc = jnp.zeros((8, 128), f32)
    for s in range(16):
        acc = acc + jnp.where(w * 8 + z == s, total, peers[s])
    out_ref[0] = acc
    out_ref[1] = half[0] + half[1]

    for cp in copies:
        cp.wait_send()
    for step in range(4):
        arrival(tiles(z, c), up_send.at[step])
        arrival(rows(z, c), ut_send.at[step])
        if step < 3:
            arrival(tiles(z, c), dn_send.at[step])
            arrival(rows(z, c), dt_send.at[step])
    for f in range(8):
        arrival(tiles(z, c), ef_send.at[f])
        arrival(rows(z, c), tf_send.at[f])


def mega(kq, freq, kp, lat, rs, eg, et):
    f32, bf16 = jnp.float32, jnp.bfloat16
    smem = pl.BlockSpec(memory_space=pltpu.SMEM)
    vmem = pl.BlockSpec(memory_space=pltpu.VMEM)
    dma = pltpu.SemaphoreType.DMA
    return pl.pallas_call(
        mega_kernel,
        out_shape=jax.ShapeDtypeStruct((2, 8, 128), f32),
        in_specs=[smem, smem] + [vmem] * 5,
        out_specs=vmem,
        scratch_shapes=[
            pltpu.VMEM((4, 2, 4, 48, 256), bf16), pltpu.VMEM((256, NB, 128), bf16), pltpu.VMEM((256, 128), f32),
            pltpu.VMEM((512, NR * NB), f32), pltpu.VMEM((2048, 384), f32),
            pltpu.VMEM((384, NR * NB), bf16), pltpu.VMEM((384, NR * NB), bf16), pltpu.VMEM((8, 1536, 256), f32),
            pltpu.VMEM((4, 256, 256), bf16), pltpu.VMEM((4, NV * NB, 256), f32), pltpu.VMEM((8 * NB, 256), f32),
            pltpu.VMEM((NV, 8, 128), f32), pltpu.VMEM((8 * NB, 128), f32),
            pltpu.VMEM((16, 8, 128), f32), pltpu.VMEM((16, 8, 128), f32), pltpu.VMEM((8, 128), f32),
            pltpu.VMEM((16, 8, 128), f32), pltpu.VMEM((2, 8, 128), f32),
            dma((3,)), dma((15,)), dma((15,)), dma((15,)), dma((15,)), dma((15,)), dma((15,)),
            dma((4,)), dma((4,)), dma((3,)), dma((3,)), dma((4,)), dma((4,)), dma((3,)), dma((3,)),
            dma((4,)), dma((4,)), dma((8,)), dma((8,)), dma((8,)), dma((8,)),
            dma((15,)), dma((15,)), dma((15,)), dma((15,)), dma((1,)), dma((1,))],
        compiler_params=pltpu.CompilerParams(collective_id=0, has_side_effects=True, vmem_limit_bytes=60 << 20),
        name="linewidths",
    )(kq, freq, kp, lat, rs, eg, et)


def on_device(coupling, rotation, freq, eigvec, energies, window, kq_index, kpoints, lattice):
    f32, bf16 = jnp.float32, jnp.bfloat16
    coup = coupling.reshape(4, 2, NM, NB, NB)
    rotated = jnp.einsum("qrcij,qcv->qrvij", coup, rotation, preferred_element_type=f32).astype(bf16)
    rs = rotated.reshape(4, 2, 4, NV, NB, NB).transpose(0, 2, 1, 5, 3, 4).reshape(4, 4, 48, NV, NB)
    low = jnp.pad(rs[:, :, :, :5].reshape(4, 4, 48, 120), ((0, 0), (0, 0), (0, 0), (0, 8)))
    high = jnp.pad(rs[:, :, :, 5:].reshape(4, 4, 48, 96), ((0, 0), (0, 0), (0, 0), (0, 32)))
    rs = jnp.concatenate([low, high], axis=-1)
    inside = jnp.arange(NB)[None, None, :] < window[:, None, None]
    eg = jnp.pad(jnp.where(inside, eigvec, jnp.zeros((), bf16)).reshape(8, 4, NB, NB), ((0, 0), (0, 0), (0, 0), (0, 8)))
    eg = eg.transpose(0, 2, 1, 3).reshape(8, NB, 128)
    et = jnp.pad(energies, ((0, 0), (0, 8))).reshape(8, 128)
    out = mega(kq_index, freq, kpoints.T, lattice, rs, eg, et)
    norm = 1.0 / (math.sqrt(2.0 * math.pi) * SIGMA)
    electron = out[0, :, :96].reshape(8, 3, 32).transpose(2, 1, 0).reshape(32, NB) * (norm / 55296.0)
    phonon = out[1, :, :32].reshape(8, 16, 2).transpose(1, 2, 0).reshape(16, 16)[:, :NV].reshape(4, NM) * (norm / 24576.0)
    return electron, phonon


def solution(mesh):
    return jax.shard_map(
        on_device,
        mesh=mesh,
        in_specs=(
            P("pb", ("ka", "row"), None),
            P("pb", None, None),
            P("pb", None),
            P(("ka", "row"), None, None),
            P(("ka", "row"), None),
            P(("ka", "row")),
            P("pb", None),
            P(),
            P(),
        ),
        out_specs=(P(("ka", "row"), None), P("pb", None)),
        check_vma=False,
    )
```

time: 555 us -> 99.7 us (0.18); the launches traced: 544 us -> 99.4 us
  blocking collectives: 353 us -> 0 us
  matrix products: 101 us -> 0.44 us
  Pallas kernels: 0 us -> 82.2 us
  local copies, waits for them, and re-layouts: 63.2 us -> 14.1 us
  between operations: 14.9 us -> 0.81 us
  waiting for transfers between devices: 8.77 us -> 0 us
    psum x2 -> x0, blocking collectives: 200 us -> none  [the longest x1 149 us: on_device(): phonon = lax.psum(phon_local, ('ka', 'row'))]
    dot_general x3 -> x0, matrix products: 101 us -> none  [the longest x1 69.3 us: block_terms(): jnp.einsum('imc,binc->bmnc', eig_kq, right, preferred_element_type=jnp.fl...]
    pallas_call x0 -> x1, Pallas kernels: none -> 82.2 us  [mega(): pl.pallas_call(mega_kernel, out_shape=jax.ShapeDtypeStruct((2, 8, 128), f...]
    all_gather x1 -> x0, blocking collectives: 79.1 us -> none  [on_device(): lax.all_gather(energies, ('ka', 'row'), axis=0, tiled=True)]
    unnamed x1 -> x0, blocking collectives: 73.2 us -> none
    reshape x3 -> x7, local copies, waits for them, and re-layouts: 47.4 us -> 7.47 us  [the longest x2 4.86 us: on_device(): coup = coupling.reshape(4, 2, NM, NB, NB)]
    all_gather x2 -> x0, waiting for transfers between devices: 8.73 us -> none  [the longest x1 8.73 us: on_device(): coup_full = lax.all_gather(coupling, ('ka', 'row'), axis=1, tiled=True)]
    unnamed x14 -> x13, local copies, waits for them, and re-layouts: 7.06 us -> 0.96 us
  transfers between devices with their start and end apart: 2 -> 0, of which waited for: 1 -> 0; matrix products, arithmetic and copies ran while one was open for 3% -> 0% of each run, Pallas kernels for 0% -> 0%
where the time goes in v2:
time: 99.7 us; the launch traced here: 99.4 us
  Pallas kernels  82.2 us (82%)
  local copies, waits for them, and re-layouts  14.1 us (14%)
  other arithmetic  1.8 us (2%)
    pallas_call x1, Pallas kernels, mega(): pl.pallas_call(mega_kernel, out_shape=jax.ShapeDtypeStruct((2, 8, 128), f...  82.2 us
    reshape x2, local copies, waits for them, and re-layouts, on_device(): coup = coupling.reshape(4, 2, NM, NB, NB)  4.86 us

profile of v2, /device:TPU:1, one launch (start us, length us, event | category | flops | bytes accessed | tf_op | source)
XLA Modules:
  0.0 99.4 jit_solution(6197821654832124176)
XLA Ops:
  0.6 3.4 %reshape.60 = bf16[4,2,36,24,24]{4,3,2,1,0:T(8,128)(2,1)S(1)} reshape(bf16[4,2,20736]{2,1,0:T(2,128)(2,1)} %param.9) | data formatting | bytes 663552 | tf_op jit(solution)/shard_map/reshape | solution.py:334
  4.0 0.0 copy-start.1
  4.0 1.5 %copy.30 = bf16[4,2,36,24,24]{2,4,3,1,0:T(8,128)(2,1)S(1)} copy(bf16[4,2,36,24,24]{4,3,2,1,0:T(8,128)(2,1)S(1)} %reshape.60) | data formatting | bytes 663552 | tf_op jit(solution)/shard_map/reshape | solution.py:334
  5.5 0.4 fusion.3
  6.0 0.2 convert_bitcast_fusion
  6.2 1.7 %copy.31 = bf16[4,2,36,24,24]{4,3,2,1,0:T(8,128)(2,1)S(1)} copy(bf16[4,2,36,24,24]{2,4,3,1,0:T(8,128)(2,1)S(1)} %convert_bitcast_fusion) | data formatting | bytes 663552 | tf_op jit(solution)/shard_map/convert_element_type | solution.py:335
  7.8 1.6 %copy.32 = bf16[4,4,2,24,9,24]{3,2,5,4,1,0:T(2,128)(2,1)S(1)} copy(bf16[4,4,2,24,9,24]{3,5,4,1,2,0:T(8,128)(2,1)S(1)} %bitcast.27) | data formatting | bytes 663552 | tf_op jit(solution)/shard_map/transpose | solution.py:336
  9.4 0.8 reshape.62
  10.2 0.0 copy-start
  10.2 0.1 slice.20
  10.3 0.0 copy-start.4
  10.3 0.2 copy.33
  10.6 0.0 copy-start.2
  10.6 0.0 copy-start.3
  10.6 0.2 copy.34
  10.8 0.8 fusion.2.rs_ref
  11.6 0.2 copy.35
  11.8 0.1 iota_compare_fusion.2
  11.9 0.1 copy.36
  12.0 0.8 reshape.66.eg_ref
  12.8 0.1 copy.43
  12.9 0.7 reshape.67.et_ref
  13.5 0.7 copy.38.lat_ref
  14.2 82.2 %linewidths.1 = f32[2,8,128]{2,1,0:T(8,128)} custom-call(s32[4,1024]{1,0:T(4,128)} %kq_ref.1, f32[4,36]{1,0:T(4,128)} %freq_ref.1, f32[3,1024]{1,0:T(4,128)} %bitcast.35, s32[64,3]{1,0:T(8,128)} %copy.38.lat_ref, bf16[4,4,48,256]{3,2,1,0:T(8,128)(2,1)} %fusion.2.rs_ref, bf16[8,24,128]{2,1,0:T(8,128)(2,1)} %reshape.66.eg_ref, f32[8,128]{1,0:T(8,128)} %reshape.67.et_ref), custom_call_target="tpu_custom_call" | custom-call | tf_op jit(solution)/shard_map/linewidths/pallas_call | solution.py:310
  96.5 0.7 slice.18
  97.2 0.1 copy.40
  97.2 0.1 copy.41
  97.3 0.1 copy.42
  97.4 0.7 mul.31
  98.1 0.7 slice_multiply_fusion.1
  98.7 0.1 mul.26
  98.8 0.6 copy.47
  (10 shorter events, 0.1 us)
Async XLA Ops:
  4.0 1.5 %copy-start.1 = (bf16[4,36,36]{2,0,1:T(4,128)(2,1)S(1)}, bf16[4,36,36]{2,0,1:T(4,128)(2,1)}, u32[]{:S(2)}) copy-start(bf16[4,36,36]{2,0,1:T(4,128)(2,1)} %param.10) | copy-start | bytes 31108
  10.2 1.4 %copy-start = (bf16[32,24,24]{0,2,1:T(8,128)(2,1)S(1)}, bf16[32,24,24]{0,2,1:T(8,128)(2,1)}, u32[]{:S(2)}) copy-start(bf16[32,24,24]{0,2,1:T(8,128)(2,1)} %param.12) | copy-start | bytes 110596
  10.3 1.5 %copy-start.4 = (s32[32]{0:T(128)S(1)}, s32[32]{0:T(128)}, u32[]{:S(2)}) copy-start(s32[32]{0:T(128)} %param.14) | copy-start | bytes 388
  10.6 2.2 %copy-start.2 = (f32[32,24]{0,1:T(8,128)S(1)}, f32[32,24]{0,1:T(8,128)}, u32[]{:S(2)}) copy-start(f32[32,24]{0,1:T(8,128)} %param.13) | copy-start | bytes 9220
  10.6 3.0 %copy-start.3 = (s32[64,3]{0,1:T(4,128)S(1)}, s32[64,3]{0,1:T(4,128)}, u32[]{:S(2)}) copy-start(s32[64,3]{0,1:T(4,128)} %param.17) | copy-start | bytes 2308

commit v3 on v2

--- a/solution.py
+++ b/solution.py
@@ -121,6 +121,35 @@
         el_ref[b] = out
 
 
+def rotate(coup_ref, rot_ref, sp, us, rs_ref):
+    f32, bf16 = jnp.float32, jnp.bfloat16
+    row = lax.broadcasted_iota(jnp.int32, (128, 1), 0)
+    v = row % NM
+    s = v % NV
+    far = jnp.where(s >= 5, 1, 0)
+    column = 256 * (v // NV) + 128 * far + NB * (s - 5 * far) + row // NM
+    column = jnp.where(row < 3 * NM, column, -1024)
+    lanes = lax.broadcasted_iota(jnp.int32, (128, 1024), 1)
+    for g in range(8):
+        sp[128 * g:128 * g + 128, :] = jnp.where(lanes == column + 3 * g, 1.0, 0.0).astype(bf16)
+    rot = rot_ref[...].astype(f32)
+    for q in range(4):
+        rq = jnp.concatenate([rot[:, q, :], jnp.zeros((NM, 128 - NM), f32)], axis=1)
+        rp = [(pltpu.roll(rq, NM * a, 1) if a else rq).astype(bf16) for a in range(3)]
+        for r in range(2):
+            ct = jnp.transpose(coup_ref[q, r].astype(f32))
+            u = jnp.zeros((8 * NB, 128), f32)
+            for a in range(3):
+                rows = jnp.concatenate([ct[NB * (3 * g + a):NB * (3 * g + a) + NB] for g in range(8)], axis=0)
+                u = u + jnp.dot(rows.astype(bf16), rp[a], preferred_element_type=f32)
+            for g in range(8):
+                us[NB * (2 * q + r):NB * (2 * q + r) + NB, 128 * g:128 * g + 128] = u[NB * g:NB * g + NB]
+    out = jnp.dot(us[...].astype(bf16), sp[...], preferred_element_type=f32).astype(bf16)
+    for q in range(4):
+        for b in range(4):
+            rs_ref[q, b] = out[48 * q:48 * q + 48, 256 * b:256 * b + 256]
+
+
 def place():
     ka, pb, row = lax.axis_index("ka"), lax.axis_index("pb"), lax.axis_index("row")
     return ka // 2, ka % 2, row, pb // 8, pb % 8
@@ -130,9 +159,9 @@
     return {"ka": 2 * y + core, "pb": 8 * y_lo + z, "row": x}
 
 
-def phases(y_unused, c, kp_ref, lat_ref, widen, pscr):
+def phases(c, kp_ref, lat_ref, widen, pscr):
     f32 = jnp.float32
-    lat = lat_ref[...].astype(f32)
+    lat = jnp.transpose(jnp.concatenate([lat_ref[...].astype(f32), jnp.zeros((5, NR), f32)], axis=0))
     for u in range(4):
         cols = pl.ds(pl.multiple_of(256 * u + 128 * c, 128), 128)
         arg = (lat[:, 0:1] * kp_ref[0:1, cols] + lat[:, 1:2] * kp_ref[1:2, cols]
@@ -142,8 +171,8 @@
             ph, widen, (((0,), (0,)), ((), ())), preferred_element_type=f32)
 
 
-def mega_kernel(kq_ref, freq_ref, kp_ref, lat_ref, rs_ref, eg_ref, et_ref, out_ref,
-                rt, eig, etab, pscr, etscr, wa, wb, xscr, bds, ybufs, aes, phacc, acc_ref,
+def mega_kernel(kq_ref, freq_ref, kp_ref, lat_ref, coup_ref, rot_ref, eg_ref, et_ref,
+                electron_ref, phonon_ref, sp, us, rs_ref, rt, eig, etab, pscr, etscr, wa, wb, xscr, bds, ybufs, aes, phacc, acc_ref,
                 el, got, mine, peers, half,
                 own, r_send, r_recv, t_send, t_recv, e_send, e_recv,
                 up_send, up_recv, dn_send, dn_recv, ut_send, ut_recv, dt_send, dt_recv,
@@ -169,10 +198,10 @@
     local = [
         pltpu.make_async_copy(eg_ref.at[z], eig.at[32 * z + 16 * c + me], own.at[0]),
         pltpu.make_async_copy(et_ref.at[pl.ds(z, 1)], etab.at[pl.ds(32 * z + 16 * c + me, 1)], own.at[1]),
-        pltpu.make_async_copy(rs_ref.at[y, x], rt.at[y, c, x], own.at[2]),
     ]
     for cp in local:
         cp.start()
+    rotate(coup_ref, rot_ref, sp, us, rs_ref)
     pl.semaphore_wait(barrier, 31)
 
     copies = []
@@ -199,8 +228,10 @@
     for n, (yy, xx, target) in enumerate(plane):
         copies.append(send(rs_ref.at[yy, xx], rt.at[y, c, x], r_send.at[n], r_recv.at[n], target))
 
+    local.append(pltpu.make_async_copy(rs_ref.at[y, x], rt.at[y, c, x], own.at[2]))
+    local[2].start()
     spread, widen = constants()
-    phases(y, c, kp_ref, lat_ref, widen, pscr)
+    phases(c, kp_ref, lat_ref, widen, pscr)
     bds[...] = jnp.zeros_like(bds)
     phacc[...] = jnp.zeros_like(phacc)
     acc_ref[...] = jnp.zeros_like(acc_ref)
@@ -286,8 +317,20 @@
     acc = jnp.zeros((8, 128), f32)
     for s in range(16):
         acc = acc + jnp.where(w * 8 + z == s, total, peers[s])
-    out_ref[0] = acc
-    out_ref[1] = half[0] + half[1]
+    norm = 1.0 / (math.sqrt(2.0 * math.pi) * SIGMA)
+    acc = jnp.concatenate([acc, pltpu.roll(acc, 96, 1), pltpu.roll(acc, 64, 1)], axis=0)
+    electron_ref[...] = acc[:, 0:32] * (norm / 55296.0)
+    both = half[0] + half[1]
+    owner = lax.broadcasted_iota(jnp.int32, (8, 128), 0)
+    spot = lax.broadcasted_iota(jnp.int32, (128, 128), 0)
+    mode = lax.broadcasted_iota(jnp.int32, (128, 128), 1)
+    result = jnp.zeros((8, 128), f32)
+    for s in range(8 if NV > 8 else NV):
+        line = jnp.where(lane // 8 == owner, both[s:s + 1], 0.0)
+        inner = 8 * (spot % 2) + s
+        to = jnp.where((inner < NV) & (mode == NV * (spot // 2 % 4) + inner), 1.0, 0.0).astype(f32)
+        result = result + jnp.dot(line, to, preferred_element_type=f32, precision=lax.Precision.HIGHEST)
+    phonon_ref[...] = result[0:4, 0:NM] * (norm / 24576.0)
 
     for cp in copies:
         cp.wait_send()
@@ -302,17 +345,18 @@
         arrival(rows(z, c), tf_send.at[f])
 
 
-def mega(kq, freq, kp, lat, rs, eg, et):
+def mega(kq, freq, kp, lat, coup, rot, eg, et):
     f32, bf16 = jnp.float32, jnp.bfloat16
     smem = pl.BlockSpec(memory_space=pltpu.SMEM)
     vmem = pl.BlockSpec(memory_space=pltpu.VMEM)
     dma = pltpu.SemaphoreType.DMA
     return pl.pallas_call(
         mega_kernel,
-        out_shape=jax.ShapeDtypeStruct((2, 8, 128), f32),
-        in_specs=[smem, smem] + [vmem] * 5,
-        out_specs=vmem,
+        out_shape=(jax.ShapeDtypeStruct((NB, 32), f32), jax.ShapeDtypeStruct((4, NM), f32)),
+        in_specs=[smem, smem] + [vmem] * 6,
+        out_specs=(vmem, vmem),
         scratch_shapes=[
+            pltpu.VMEM((1024, 1024), bf16), pltpu.VMEM((192, 1024), f32), pltpu.VMEM((4, 4, 48, 256), bf16),
             pltpu.VMEM((4, 2, 4, 48, 256), bf16), pltpu.VMEM((256, NB, 128), bf16), pltpu.VMEM((256, 128), f32),
             pltpu.VMEM((512, NR * NB), f32), pltpu.VMEM((2048, 384), f32),
             pltpu.VMEM((384, NR * NB), bf16), pltpu.VMEM((384, NR * NB), bf16), pltpu.VMEM((8, 1536, 256), f32),
@@ -326,26 +370,18 @@
             dma((15,)), dma((15,)), dma((15,)), dma((15,)), dma((1,)), dma((1,))],
         compiler_params=pltpu.CompilerParams(collective_id=0, has_side_effects=True, vmem_limit_bytes=60 << 20),
         name="linewidths",
-    )(kq, freq, kp, lat, rs, eg, et)
+    )(kq, freq, kp, lat, coup, rot, eg, et)
 
 
 def on_device(coupling, rotation, freq, eigvec, energies, window, kq_index, kpoints, lattice):
     f32, bf16 = jnp.float32, jnp.bfloat16
-    coup = coupling.reshape(4, 2, NM, NB, NB)
-    rotated = jnp.einsum("qrcij,qcv->qrvij", coup, rotation, preferred_element_type=f32).astype(bf16)
-    rs = rotated.reshape(4, 2, 4, NV, NB, NB).transpose(0, 2, 1, 5, 3, 4).reshape(4, 4, 48, NV, NB)
-    low = jnp.pad(rs[:, :, :, :5].reshape(4, 4, 48, 120), ((0, 0), (0, 0), (0, 0), (0, 8)))
-    high = jnp.pad(rs[:, :, :, 5:].reshape(4, 4, 48, 96), ((0, 0), (0, 0), (0, 0), (0, 32)))
-    rs = jnp.concatenate([low, high], axis=-1)
     inside = jnp.arange(NB)[None, None, :] < window[:, None, None]
     eg = jnp.pad(jnp.where(inside, eigvec, jnp.zeros((), bf16)).reshape(8, 4, NB, NB), ((0, 0), (0, 0), (0, 0), (0, 8)))
     eg = eg.transpose(0, 2, 1, 3).reshape(8, NB, 128)
     et = jnp.pad(energies, ((0, 0), (0, 8))).reshape(8, 128)
-    out = mega(kq_index, freq, kpoints.T, lattice, rs, eg, et)
-    norm = 1.0 / (math.sqrt(2.0 * math.pi) * SIGMA)
-    electron = out[0, :, :96].reshape(8, 3, 32).transpose(2, 1, 0).reshape(32, NB) * (norm / 55296.0)
-    phonon = out[1, :, :32].reshape(8, 16, 2).transpose(1, 2, 0).reshape(16, 16)[:, :NV].reshape(4, NM) * (norm / 24576.0)
-    return electron, phonon
+    electron, phonon = mega(kq_index, freq, kpoints.T, lattice.T, coupling.reshape(4, 2, NM, NB * NB),
+                            rotation.transpose(1, 0, 2), eg, et)
+    return electron.T, phonon
 
 
 def solution(mesh):

time: 99.7 us -> 91.3 us (0.916)
  local copies, waits for them, and re-layouts: 14.1 us -> 7.31 us
  other arithmetic: 1.8 us -> 0.11 us
    reshape x5 -> x1, local copies, waits for them, and re-layouts: 6.04 us -> 1.25 us  [on_device(): coupling.reshape(4, 2, NM, NB * NB)]
    unnamed x13 -> x10, local copies, waits for them, and re-layouts: 0.96 us -> 4.5 us
    convert_element_type x1 -> x0, local copies, waits for them, and re-layouts: 1.66 us -> none  [on_device(): jnp.einsum('qrcij,qcv->qrvij', coup, rotation, preferred_element_type=f32)]
    transpose x2 -> x0, local copies, waits for them, and re-layouts: 1.64 us -> none  [the longest x1 1.57 us: on_device(): rotated.reshape(4, 2, 4, NV, NB, NB).transpose(0, 2, 1, 5, 3, 4)]
    mul x4 -> x0, local copies, waits for them, and re-layouts: 1.43 us -> none  [the longest x2 0.74 us: on_device(): out[1, :, :32].reshape(8, 16, 2).transpose(1, 2, 0).reshape(16, 16)[:, :NV]]
where the time goes in v3:
time: 91.3 us; the launch traced here: 91 us
  Pallas kernels  82.9 us (91%)
  local copies, waits for them, and re-layouts  7.31 us (8%)
    pallas_call x1, Pallas kernels, mega(): pl.pallas_call(mega_kernel, out_shape=(jax.ShapeDtypeStruct((NB, 32), f32...  82.9 us
    unnamed x10, local copies, waits for them, and re-layouts  4.5 us

profile of v3, /device:TPU:1, one launch (start us, length us, event | category | flops | bytes accessed | tf_op | source)
XLA Modules:
  0.0 91.0 jit_solution(2883562147320818800)
XLA Ops:
  0.6 0.0 copy-start.2
  0.6 0.6 copy-done.2
  1.3 0.1 iota_compare_fusion
  1.4 0.8 copy.16
  2.1 0.7 reshape.40.et_ref
  2.8 1.1 %copy.13 = bf16[32,24,24]{2,1,0:T(8,128)(2,1)S(1)} copy(bf16[32,24,24]{0,2,1:T(8,128)(2,1)} %param.12) | data formatting | bytes 73728 | tf_op args[3]
  4.0 0.0 copy-start
  4.0 0.1 copy.14
  4.1 0.8 reshape.39.eg_ref
  4.8 0.1 copy-done
  5.0 1.2 %reshape.37.coup_ref = bf16[4,2,36,576]{3,2,1,0:T(8,128)(2,1)} reshape(bf16[4,2,20736]{2,1,0:T(2,128)(2,1)S(1)} %copy-done) | data formatting | bytes 663552 | tf_op jit(solution)/shard_map/reshape | solution.py:382
  6.2 82.9 %linewidths.1 = (f32[24,32]{1,0:T(8,128)}, f32[4,36]{1,0:T(4,128)}) custom-call(s32[4,1024]{1,0:T(4,128)} %kq_ref.1, f32[4,36]{1,0:T(4,128)} %freq_ref.1, f32[3,1024]{1,0:T(4,128)} %bitcast.9, s32[3,64]{1,0:T(4,128)} %bitcast.11, bf16[4,2,36,576]{3,2,1,0:T(8,128)(2,1)} %reshape.37.coup_ref, bf16[36,4,36]{2,1,0:T(4,128)(2,1)} %bitcast.8, ...), custom_call_target="tpu_custom_call" | custom-call | tf_op jit(solution)/shard_map/linewidths/pallas_call | solution.py:353
  89.1 0.0 copy-start.1
  89.1 1.3 %copy.19 = f32[32,24]{0,1:T(8,128)} copy(f32[32,24]{0,1:T(8,128)} %bitcast.10) | data formatting | bytes 6144
  90.4 0.0 copy-done.1
  90.4 0.6 copy.20
  (3 shorter events, 0.1 us)
Async XLA Ops:
  0.6 0.7 copy-start.2
  4.0 1.0 %copy-start = (bf16[4,2,20736]{2,1,0:T(2,128)(2,1)S(1)}, bf16[4,2,20736]{2,1,0:T(2,128)(2,1)}, u32[]{:S(2)}) copy-start(bf16[4,2,20736]{2,1,0:T(2,128)(2,1)} %param.9) | copy-start | bytes 995332
  89.1 1.3 %copy-start.1 = (f32[4,36]{1,0:T(4,128)S(1)}, f32[4,36]{1,0:T(4,128)}, u32[]{:S(2)}) copy-start(f32[4,36]{1,0:T(4,128)} %get-tuple-element.9) | copy-start | bytes 1732

commit v4 on v3

--- a/solution.py
+++ b/solution.py
@@ -11,6 +11,7 @@
 KT = 0.2
 NB, NM, NR = 24, 36, 64
 NV = 9
+SHARP = math.sqrt(1.0 / (2.0 * SIGMA * SIGMA * math.log(2.0)))
 PITCH = 32
 VSLOT = [(v // 5, v % 5) for v in range(NV)]
 
@@ -26,7 +27,7 @@
     return spread, widen
 
 
-def right_stage(t, c, rt_ref, eig_ref, spread, pscr, etscr, wbufs, xscr):
+def right_steps(i, t, c, rt_ref, eig_ref, spread, pscr, etscr, wbufs, xscr):
     f32, bf16 = jnp.float32, jnp.bfloat16
     tt = jnp.concatenate([eig_ref[32 * t + 16 * c + b] for b in range(16)], axis=1)
     etscr[...] = lax.dot_general(tt, spread, (((0,), (0,)), ((), ())), preferred_element_type=f32)
@@ -40,13 +41,16 @@
                 p = pscr[pl.ds((k // 4) * 32 + 4 * t + k % 4, 1), :]
                 parts.append(jnp.concatenate([ek * p[:, 384 * a:384 * a + 384] for a in range(4)], axis=1))
             wbuf[48 * pair:48 * pair + 48, :] = jnp.concatenate(parts, axis=0).astype(bf16)
-        xscr[t, 384 * sub:384 * sub + 384, :] = jnp.dot(wbuf[...], rt_ref[...].reshape(NR * NB, 256), preferred_element_type=f32)
-
-
-def final_stage(t, c, q, vq, kq_ref, freq_ref, eig_ref, etab_ref, xscr, bds, ybufs, aes, phacc, acc_ref):
+        xscr[i, 384 * sub:384 * sub + 384, :] = jnp.dot(wbuf[...], rt_ref[...].reshape(NR * NB, 256), preferred_element_type=f32)
+        yield
+
+
+def final_steps(i, t, c, q, vq, kq_ref, freq_ref, eig_ref, etab_ref, xscr, bds, ybufs, aes, phacc, acc_ref):
     f32, bf16 = jnp.float32, jnp.bfloat16
     lane = lax.broadcasted_iota(jnp.int32, (1, 128), 1)
+    freqs = [freq_ref[q, NV * vq + v] * SHARP for v in range(NV)]
     ekt = jnp.transpose(etab_ref[pl.ds(pl.multiple_of(32 * t + 16 * c, 16), 16), :])
+    sums = [jnp.zeros((8, 128), f32) for _ in range(NV)]
     for g in range(8):
         bd, ybuf = bds.at[g % 4], ybufs.at[g % 4]
         eps = []
@@ -70,7 +74,7 @@
             for k4 in range(4):
                 k = 8 * g + 4 * h + k4
                 for vt in range(2):
-                    x = xscr[t, NB * k:NB * k + NB, 128 * vt:128 * vt + 128]
+                    x = xscr[i, NB * k:NB * k + NB, 128 * vt:128 * vt + 128]
                     xs[vt][k4] = pltpu.roll(x, PITCH * k4, 1) if k4 else x
             for v in range(NV):
                 vt, s = VSLOT[v]
@@ -87,17 +91,20 @@
             ek = jnp.zeros((NB, 128), f32)
             for k4 in range(4):
                 ek = jnp.where(lane // PITCH == k4, ekt[PITCH * k4:PITCH * k4 + NB, b:b + 1], ek)
-            diff = eps[h] - ek
+            diff = (eps[h] - ek) * SHARP
             occ = jax.nn.sigmoid(ek * (-1.0 / KT)) - jax.nn.sigmoid(eps[h] * (-1.0 / KT))
             acc = jnp.zeros((NB, 128), f32)
             for v in range(NV):
                 zv = zz[NB * v:NB * v + NB, 128 * h:128 * h + 128]
-                d = diff - freq_ref[q, NV * vq + v]
-                st = zv * zv * jnp.exp(d * d * (-1.0 / (2 * SIGMA * SIGMA)))
+                d = diff - freqs[v]
+                st = zv * zv * jnp.exp2(-(d * d))
                 acc = acc + st
                 so = st * occ
-                phacc[v] += so[0:8] + so[8:16] + so[16:24]
+                sums[v] = sums[v] + (so[0:8] + so[8:16] + so[16:24])
             aes[NB * g:NB * g + NB, 128 * h:128 * h + 128] = acc
+        yield
+    for v in range(NV):
+        phacc[v] += sums[v]
     r3 = lax.broadcasted_iota(jnp.int32, (256, 128), 0)
     c3 = lax.broadcasted_iota(jnp.int32, (256, 128), 1)
     fold = jnp.where(c3 == (r3 // 128) * 64 + 4 * t + (r3 % 128) // PITCH, 1.0, 0.0).astype(f32)
@@ -118,7 +125,15 @@
             piece = jnp.where(lane // 64 == b % 2, acc_ref[a:a + 8, :], 0.0)
             shift = (32 * u + 64 * (b % 2)) % 128
             out = out + (pltpu.roll(piece, shift, 1) if shift else piece)
-        el_ref[b] = out
+        el_ref[4 * (b % 4) + b // 4] = out
+
+
+def run(*steps):
+    steps = list(steps)
+    while steps:
+        for s in list(steps):
+            if next(s, "end") == "end":
+                steps.remove(s)
 
 
 def rotate(coup_ref, rot_ref, sp, us, rs_ref):
@@ -150,6 +165,26 @@
             rs_ref[q, b] = out[48 * q:48 * q + 48, 256 * b:256 * b + 256]
 
 
+def own_slice(z, ev_ref, en_ref, win_ref):
+    f32, bf16 = jnp.float32, jnp.bfloat16
+    lane = lax.broadcasted_iota(jnp.int32, (1, 128), 1)
+    pick = lax.broadcasted_iota(jnp.int32, (32, 128), 0) == 4 * z + lane // PITCH
+    lim = jnp.dot(jnp.broadcast_to(win_ref[...], (8, 32)).astype(bf16), jnp.where(pick, 1.0, 0.0).astype(bf16),
+                  preferred_element_type=f32)[0:1]
+    band = lane % PITCH
+    wide = jnp.dot(ev_ref[...], jnp.where(pick, 1.0, 0.0).astype(bf16), preferred_element_type=f32)
+    row = lax.broadcasted_iota(jnp.int32, (NB * NB, 128), 0)
+    keep = (row % NB == band) & (band.astype(f32) < lim)
+    r4 = lax.broadcasted_iota(jnp.int32, (NB, NB * NB), 0)
+    c4 = lax.broadcasted_iota(jnp.int32, (NB, NB * NB), 1)
+    gather = jnp.where(c4 // NB == r4, 1.0, 0.0).astype(bf16)
+    vectors = jnp.dot(gather, jnp.where(keep, wide, 0.0).astype(bf16), preferred_element_type=f32)
+    levels = jnp.dot(en_ref[...], jnp.where(pick, 1.0, 0.0).astype(f32), preferred_element_type=f32,
+                     precision=lax.Precision.HIGHEST)
+    levels = jnp.where(lax.broadcasted_iota(jnp.int32, (NB, 128), 0) == band, levels, 0.0)
+    return vectors.astype(bf16), jnp.sum(levels, axis=0, keepdims=True)
+
+
 def place():
     ka, pb, row = lax.axis_index("ka"), lax.axis_index("pb"), lax.axis_index("row")
     return ka // 2, ka % 2, row, pb // 8, pb % 8
@@ -171,9 +206,9 @@
             ph, widen, (((0,), (0,)), ((), ())), preferred_element_type=f32)
 
 
-def mega_kernel(kq_ref, freq_ref, kp_ref, lat_ref, coup_ref, rot_ref, eg_ref, et_ref,
-                electron_ref, phonon_ref, sp, us, rs_ref, rt, eig, etab, pscr, etscr, wa, wb, xscr, bds, ybufs, aes, phacc, acc_ref,
-                el, got, mine, peers, half,
+def mega_kernel(kq_ref, freq_ref, kp_ref, lat_ref, coup_ref, rot_ref, ev_ref, en_ref, win_ref,
+                electron_ref, phonon_ref, sp, us, rs_ref, rt, eig, etab, pscr, etscr, wa, wb, xa, xb, bds, ybufs, aes, phacc, acc_ref,
+                el, got, tiles2, got2, mine, peers, half,
                 own, r_send, r_recv, t_send, t_recv, e_send, e_recv,
                 up_send, up_recv, dn_send, dn_recv, ut_send, ut_recv, dt_send, dt_recv,
                 rf_send, rf_recv, ef_send, ef_recv, tf_send, tf_recv,
@@ -195,12 +230,8 @@
     for target in [o[2] for o in plane] + column + [partner]:
         pl.semaphore_signal(barrier, inc=1, device_id=target, device_id_type=pl.DeviceIdType.MESH)
 
-    local = [
-        pltpu.make_async_copy(eg_ref.at[z], eig.at[32 * z + 16 * c + me], own.at[0]),
-        pltpu.make_async_copy(et_ref.at[pl.ds(z, 1)], etab.at[pl.ds(32 * z + 16 * c + me, 1)], own.at[1]),
-    ]
-    for cp in local:
-        cp.start()
+    here = 32 * z + 16 * c + me
+    eig[here], etab[pl.ds(here, 1), :] = own_slice(z, ev_ref, en_ref, win_ref)
     rotate(coup_ref, rot_ref, sp, us, rs_ref)
     pl.semaphore_wait(barrier, 31)
 
@@ -221,15 +252,14 @@
     def rows(t, core):
         return etab.at[pl.ds(pl.multiple_of(32 * t + 16 * core, 16), 16)]
 
-    here = 32 * z + 16 * c + me
     for n, (yy, xx, target) in enumerate(plane):
-        copies.append(send(eg_ref.at[z], eig.at[here], e_send.at[n], e_recv.at[n], target))
-        copies.append(send(et_ref.at[pl.ds(z, 1)], etab.at[pl.ds(here, 1)], t_send.at[n], t_recv.at[n], target))
+        copies.append(send(eig.at[here], eig.at[here], e_send.at[n], e_recv.at[n], target))
+        copies.append(send(etab.at[pl.ds(here, 1)], etab.at[pl.ds(here, 1)], t_send.at[n], t_recv.at[n], target))
     for n, (yy, xx, target) in enumerate(plane):
         copies.append(send(rs_ref.at[yy, xx], rt.at[y, c, x], r_send.at[n], r_recv.at[n], target))
 
-    local.append(pltpu.make_async_copy(rs_ref.at[y, x], rt.at[y, c, x], own.at[2]))
-    local[2].start()
+    local = pltpu.make_async_copy(rs_ref.at[y, x], rt.at[y, c, x], own.at[0])
+    local.start()
     spread, widen = constants()
     phases(c, kp_ref, lat_ref, widen, pscr)
     bds[...] = jnp.zeros_like(bds)
@@ -257,8 +287,7 @@
     def slice_of(f):
         return (z + 8 - f) % 8 if f < 5 else (z + f - 4) % 8
 
-    for cp in local:
-        cp.wait()
+    local.wait()
     for n in range(15):
         d = n + 1
         b = (y + 4 - d // 4) % 4 * 4 + (x + 4 - d % 4) % 4
@@ -275,36 +304,61 @@
     for dy in range(4):
         arrival(rt.at[(y + 4 - dy) % 4, 1 - c], rf_recv.at[dy])
 
-    def right(i, _):
-        for step, at in ((2, 1), (3, 3), (4, 5)):
-            pl.when(i == at)(lambda step=step: ring(step))
-        t = (z + 8 + (1 - 2 * (i % 2)) * ((i + 1) // 2)) % 8
-        right_stage(t, c, rt, eig, spread, pscr, etscr, (wa, wb), xscr)
+    def slice_at(i):
+        return (z + 8 + (1 - 2 * (i % 2)) * ((i + 1) // 2)) % 8
+
+    rargs = (c, rt, eig, spread, pscr, etscr, (wa, wb))
+    fargs = (c, y, x, kq_ref, freq_ref, eig, etab)
+    sums = (bds, ybufs, aes, phacc, acc_ref)
+
+    def first(i, _):
+        for step in (2, 3, 4):
+            pl.when(i == step - 2 + step // 4)(lambda step=step: ring(step))
+        run(right_steps(i, slice_at(i), *rargs, xa))
         return 0
-    lax.fori_loop(0, 8, right, 0)
+    lax.fori_loop(0, 4, first, 0)
 
     for f in range(8):
         arrival(tiles(slice_of(f), 1 - c), ef_recv.at[f])
         arrival(rows(slice_of(f), 1 - c), tf_recv.at[f])
 
-    def final(t, _):
-        final_stage(t, c, y, x, kq_ref, freq_ref, eig, etab, xscr, bds, ybufs, aes, phacc, acc_ref)
+    def both_stages(i, _):
+        run(final_steps(i, slice_at(i), *fargs, xa, *sums), right_steps(i, slice_at(i + 4), *rargs, xb))
         return 0
-    lax.fori_loop(0, 8, final, 0)
+    lax.fori_loop(0, 4, both_stages, 0)
+
+    def last(i, _):
+        run(final_steps(i, slice_at(i + 4), *fargs, xb, *sums))
+        return 0
+    lax.fori_loop(0, 4, last, 0)
     pack_sums(phacc, acc_ref, el)
 
-    for n, (yy, xx, target) in enumerate(plane):
-        copies.append(send(el.at[yy * 4 + xx], got.at[me], a_send.at[n], a_recv.at[n], target))
-    for n in range(15):
-        d = n + 1
-        arrival(got.at[(y + 4 - d // 4) % 4 * 4 + (x + 4 - d % 4) % 4], a_recv.at[n])
+    for d in range(1, 4):
+        xx = (x + d) % 4
+        copies.append(send(el.at[pl.ds(4 * xx, 4)], got.at[pl.ds(4 * x, 4)], a_send.at[d - 1], a_recv.at[d - 1],
+                           device(y, c, xx, w, z)))
+    for d in range(1, 4):
+        arrival(got.at[pl.ds(4 * ((x + 4 - d) % 4), 4)], a_recv.at[d - 1])
     lane = lax.broadcasted_iota(jnp.int32, (8, 128), 1)
+    for yy in range(4):
+        total = jnp.zeros((8, 128), f32)
+        for s in range(4):
+            tile = jnp.where(x == s, el[4 * s + yy], got[4 * s + yy])
+            total = total + jnp.where(lane < 96, tile, 0.0)
+            phonon = jnp.where((lane == 96) | (lane == 97), tile, 0.0)
+            total = total + (pltpu.roll(phonon, 2 * s, 1) if s else phonon)
+        tiles2[yy] = total
+    for d in range(1, 4):
+        yy = (y + d) % 4
+        copies.append(send(tiles2.at[yy], got2.at[y], a_send.at[d + 2], a_recv.at[d + 2], device(yy, c, x, w, z)))
+    for d in range(1, 4):
+        arrival(got2.at[(y + 4 - d) % 4], a_recv.at[d + 2])
     total = jnp.zeros((8, 128), f32)
     phonon = jnp.zeros((8, 128), f32)
-    for s in range(16):
-        tile = jnp.where(me == s, el[s], got[s])
-        total = total + tile
-        phonon = phonon + pltpu.roll(jnp.where((lane == 96) | (lane == 97), tile, 0.0), (2 * s + 32) % 128, 1)
+    for s in range(4):
+        tile = jnp.where(y == s, tiles2[s], got2[s])
+        total = total + jnp.where(lane < 96, tile, 0.0)
+        phonon = phonon + pltpu.roll(jnp.where((lane >= 96) & (lane < 104), tile, 0.0), 32 + 8 * s, 1)
     mine[...] = total
     half[0] = phonon
     for n, target in enumerate(column):
@@ -345,7 +399,7 @@
         arrival(rows(z, c), tf_send.at[f])
 
 
-def mega(kq, freq, kp, lat, coup, rot, eg, et):
+def mega(kq, freq, kp, lat, coup, rot, ev, en, win):
     f32, bf16 = jnp.float32, jnp.bfloat16
     smem = pl.BlockSpec(memory_space=pltpu.SMEM)
     vmem = pl.BlockSpec(memory_space=pltpu.VMEM)
@@ -353,34 +407,31 @@
     return pl.pallas_call(
         mega_kernel,
         out_shape=(jax.ShapeDtypeStruct((NB, 32), f32), jax.ShapeDtypeStruct((4, NM), f32)),
-        in_specs=[smem, smem] + [vmem] * 6,
+        in_specs=[smem, smem] + [vmem] * 7,
         out_specs=(vmem, vmem),
         scratch_shapes=[
             pltpu.VMEM((1024, 1024), bf16), pltpu.VMEM((192, 1024), f32), pltpu.VMEM((4, 4, 48, 256), bf16),
             pltpu.VMEM((4, 2, 4, 48, 256), bf16), pltpu.VMEM((256, NB, 128), bf16), pltpu.VMEM((256, 128), f32),
             pltpu.VMEM((512, NR * NB), f32), pltpu.VMEM((2048, 384), f32),
-            pltpu.VMEM((384, NR * NB), bf16), pltpu.VMEM((384, NR * NB), bf16), pltpu.VMEM((8, 1536, 256), f32),
+            pltpu.VMEM((384, NR * NB), bf16), pltpu.VMEM((384, NR * NB), bf16), pltpu.VMEM((4, 1536, 256), f32), pltpu.VMEM((4, 1536, 256), f32),
             pltpu.VMEM((4, 256, 256), bf16), pltpu.VMEM((4, NV * NB, 256), f32), pltpu.VMEM((8 * NB, 256), f32),
             pltpu.VMEM((NV, 8, 128), f32), pltpu.VMEM((8 * NB, 128), f32),
-            pltpu.VMEM((16, 8, 128), f32), pltpu.VMEM((16, 8, 128), f32), pltpu.VMEM((8, 128), f32),
+            pltpu.VMEM((16, 8, 128), f32), pltpu.VMEM((16, 8, 128), f32), pltpu.VMEM((4, 8, 128), f32),
+            pltpu.VMEM((4, 8, 128), f32), pltpu.VMEM((8, 128), f32),
             pltpu.VMEM((16, 8, 128), f32), pltpu.VMEM((2, 8, 128), f32),
-            dma((3,)), dma((15,)), dma((15,)), dma((15,)), dma((15,)), dma((15,)), dma((15,)),
+            dma((1,)), dma((15,)), dma((15,)), dma((15,)), dma((15,)), dma((15,)), dma((15,)),
             dma((4,)), dma((4,)), dma((3,)), dma((3,)), dma((4,)), dma((4,)), dma((3,)), dma((3,)),
             dma((4,)), dma((4,)), dma((8,)), dma((8,)), dma((8,)), dma((8,)),
-            dma((15,)), dma((15,)), dma((15,)), dma((15,)), dma((1,)), dma((1,))],
+            dma((6,)), dma((6,)), dma((15,)), dma((15,)), dma((1,)), dma((1,))],
         compiler_params=pltpu.CompilerParams(collective_id=0, has_side_effects=True, vmem_limit_bytes=60 << 20),
         name="linewidths",
-    )(kq, freq, kp, lat, coup, rot, eg, et)
+    )(kq, freq, kp, lat, coup, rot, ev, en, win)
 
 
 def on_device(coupling, rotation, freq, eigvec, energies, window, kq_index, kpoints, lattice):
-    f32, bf16 = jnp.float32, jnp.bfloat16
-    inside = jnp.arange(NB)[None, None, :] < window[:, None, None]
-    eg = jnp.pad(jnp.where(inside, eigvec, jnp.zeros((), bf16)).reshape(8, 4, NB, NB), ((0, 0), (0, 0), (0, 0), (0, 8)))
-    eg = eg.transpose(0, 2, 1, 3).reshape(8, NB, 128)
-    et = jnp.pad(energies, ((0, 0), (0, 8))).reshape(8, 128)
     electron, phonon = mega(kq_index, freq, kpoints.T, lattice.T, coupling.reshape(4, 2, NM, NB * NB),
-                            rotation.transpose(1, 0, 2), eg, et)
+                            rotation.transpose(1, 0, 2), eigvec.transpose(1, 2, 0).reshape(NB * NB, 32), energies.T,
+                            window.reshape(1, 32))
     return electron.T, phonon
 
 

time: 91.3 us -> 87.8 us (0.962)
  the two profiles are of different devices: /device:TPU:1 before, /device:TPU:8 now
where the time goes in v4:
time: 87.8 us; the launch traced here: 87.6 us
  Pallas kernels  82.9 us (94%)
  local copies, waits for them, and re-layouts  4.12 us (5%)
    pallas_call x1, Pallas kernels, mega(): pl.pallas_call(mega_kernel, out_shape=(jax.ShapeDtypeStruct((NB, 32), f32...  82.9 us
    reshape x1, local copies, waits for them, and re-layouts, on_device(): coupling.reshape(4, 2, NM, NB * NB)  2.23 us
    unnamed x4, local copies, waits for them, and re-layouts  1.89 us

profile of v4, /device:TPU:8, one launch (start us, length us, event | category | flops | bytes accessed | tf_op | source)
XLA Modules:
  0.0 87.6 jit_solution(10306951200865009467)
XLA Ops:
  0.6 2.2 %reshape.13.coup_ref = bf16[4,2,36,576]{3,2,1,0:T(8,128)(2,1)} reshape(bf16[4,2,20736]{2,1,0:T(2,128)(2,1)} %param.9) | data formatting | bytes 663552 | tf_op jit(solution)/shard_map/reshape | solution.py:432
  2.9 82.9 %linewidths.1 = (f32[24,32]{1,0:T(8,128)}, f32[4,36]{1,0:T(4,128)}) custom-call(s32[4,1024]{1,0:T(4,128)} %kq_ref.1, f32[4,36]{1,0:T(4,128)} %freq_ref.1, f32[3,1024]{1,0:T(4,128)} %bitcast.11, s32[3,64]{1,0:T(4,128)} %bitcast.14, bf16[4,2,36,576]{3,2,1,0:T(8,128)(2,1)} %reshape.13.coup_ref, bf16[36,4,36]{2,1,0:T(4,128)(2,1)} %bitcast.10, ...), custom_call_target="tpu_custom_call" | custom-call | tf_op jit(solution)/shard_map/linewidths/pallas_call | solution.py:407
  85.7 0.0 copy-start
  85.7 1.3 %copy.13 = f32[32,24]{0,1:T(8,128)} copy(f32[32,24]{0,1:T(8,128)} %bitcast.12) | data formatting | bytes 6144
  87.0 0.0 copy-done
  87.0 0.6 copy.14
Async XLA Ops:
  85.7 1.3 %copy-start = (f32[4,36]{1,0:T(4,128)S(1)}, f32[4,36]{1,0:T(4,128)}, u32[]{:S(2)}) copy-start(f32[4,36]{1,0:T(4,128)} %get-tuple-element.9) | copy-start | bytes 1732

commit v5 on v4

--- a/solution.py
+++ b/solution.py
@@ -313,24 +313,29 @@
 
     def first(i, _):
         for step in (2, 3, 4):
-            pl.when(i == step - 2 + step // 4)(lambda step=step: ring(step))
+            pl.when(i == step - 2 + 2 * (step // 4))(lambda step=step: ring(step))
         run(right_steps(i, slice_at(i), *rargs, xa))
         return 0
-    lax.fori_loop(0, 4, first, 0)
+    lax.fori_loop(0, 5, first, 0)
 
     for f in range(8):
         arrival(tiles(slice_of(f), 1 - c), ef_recv.at[f])
         arrival(rows(slice_of(f), 1 - c), tf_recv.at[f])
 
     def both_stages(i, _):
-        run(final_steps(i, slice_at(i), *fargs, xa, *sums), right_steps(i, slice_at(i + 4), *rargs, xb))
+        run(final_steps(i, slice_at(i), *fargs, xa, *sums), right_steps(i, slice_at(i + 5), *rargs, xb))
         return 0
-    lax.fori_loop(0, 4, both_stages, 0)
+    lax.fori_loop(0, 3, both_stages, 0)
+
+    def late(i, _):
+        run(final_steps(i, slice_at(i), *fargs, xa, *sums))
+        return 0
+    lax.fori_loop(3, 5, late, 0)
 
     def last(i, _):
-        run(final_steps(i, slice_at(i + 4), *fargs, xb, *sums))
+        run(final_steps(i, slice_at(i + 5), *fargs, xb, *sums))
         return 0
-    lax.fori_loop(0, 4, last, 0)
+    lax.fori_loop(0, 3, last, 0)
     pack_sums(phacc, acc_ref, el)
 
     for d in range(1, 4):
@@ -364,16 +369,7 @@
     for n, target in enumerate(column):
         copies.append(send(mine, peers.at[w * 8 + z], b_send.at[n], b_recv.at[n], target))
     copies.append(send(half.at[0], half.at[1], p_send.at[0], p_recv.at[0], partner))
-    for n in range(15):
-        d = n + 1
-        arrival(peers.at[(w + 2 - d // 8) % 2 * 8 + (z + 8 - d % 8) % 8], b_recv.at[n])
     arrival(half.at[1], p_recv.at[0])
-    acc = jnp.zeros((8, 128), f32)
-    for s in range(16):
-        acc = acc + jnp.where(w * 8 + z == s, total, peers[s])
-    norm = 1.0 / (math.sqrt(2.0 * math.pi) * SIGMA)
-    acc = jnp.concatenate([acc, pltpu.roll(acc, 96, 1), pltpu.roll(acc, 64, 1)], axis=0)
-    electron_ref[...] = acc[:, 0:32] * (norm / 55296.0)
     both = half[0] + half[1]
     owner = lax.broadcasted_iota(jnp.int32, (8, 128), 0)
     spot = lax.broadcasted_iota(jnp.int32, (128, 128), 0)
@@ -384,7 +380,15 @@
         inner = 8 * (spot % 2) + s
         to = jnp.where((inner < NV) & (mode == NV * (spot // 2 % 4) + inner), 1.0, 0.0).astype(f32)
         result = result + jnp.dot(line, to, preferred_element_type=f32, precision=lax.Precision.HIGHEST)
-    phonon_ref[...] = result[0:4, 0:NM] * (norm / 24576.0)
+    phonon_ref[...] = result[0:4, 0:NM]
+    for n in range(15):
+        d = n + 1
+        arrival(peers.at[(w + 2 - d // 8) % 2 * 8 + (z + 8 - d % 8) % 8], b_recv.at[n])
+    acc = jnp.zeros((8, 128), f32)
+    for s in range(16):
+        acc = acc + jnp.where(w * 8 + z == s, total, peers[s])
+    acc = jnp.concatenate([acc, pltpu.roll(acc, 96, 1), pltpu.roll(acc, 64, 1)], axis=0)
+    electron_ref[...] = acc[:, 0:32]
 
     for cp in copies:
         cp.wait_send()
@@ -413,7 +417,7 @@
             pltpu.VMEM((1024, 1024), bf16), pltpu.VMEM((192, 1024), f32), pltpu.VMEM((4, 4, 48, 256), bf16),
             pltpu.VMEM((4, 2, 4, 48, 256), bf16), pltpu.VMEM((256, NB, 128), bf16), pltpu.VMEM((256, 128), f32),
             pltpu.VMEM((512, NR * NB), f32), pltpu.VMEM((2048, 384), f32),
-            pltpu.VMEM((384, NR * NB), bf16), pltpu.VMEM((384, NR * NB), bf16), pltpu.VMEM((4, 1536, 256), f32), pltpu.VMEM((4, 1536, 256), f32),
+            pltpu.VMEM((384, NR * NB), bf16), pltpu.VMEM((384, NR * NB), bf16), pltpu.VMEM((5, 1536, 256), f32), pltpu.VMEM((3, 1536, 256), f32),
             pltpu.VMEM((4, 256, 256), bf16), pltpu.VMEM((4, NV * NB, 256), f32), pltpu.VMEM((8 * NB, 256), f32),
             pltpu.VMEM((NV, 8, 128), f32), pltpu.VMEM((8 * NB, 128), f32),
             pltpu.VMEM((16, 8, 128), f32), pltpu.VMEM((16, 8, 128), f32), pltpu.VMEM((4, 8, 128), f32),
@@ -432,7 +436,8 @@
     electron, phonon = mega(kq_index, freq, kpoints.T, lattice.T, coupling.reshape(4, 2, NM, NB * NB),
                             rotation.transpose(1, 0, 2), eigvec.transpose(1, 2, 0).reshape(NB * NB, 32), energies.T,
                             window.reshape(1, 32))
-    return electron.T, phonon
+    norm = 1.0 / (math.sqrt(2.0 * math.pi) * SIGMA)
+    return electron.T * (norm / 55296.0), phonon * (norm / 24576.0)
 
 
 def solution(mesh):

time: 87.8 us -> 88.9 us (1.013)
  the two profiles are of different devices: /device:TPU:8 before, /device:TPU:1 now
where the time goes in v5:
time: 88.9 us; the launch traced here: 87.2 us
  Pallas kernels  82.4 us (93%)
  local copies, waits for them, and re-layouts  2.23 us (3%)
  other arithmetic  1.89 us (2%)
    pallas_call x1, Pallas kernels, mega(): pl.pallas_call(mega_kernel, out_shape=(jax.ShapeDtypeStruct((NB, 32), f32...  82.4 us
    reshape x1, local copies, waits for them, and re-layouts, on_device(): coupling.reshape(4, 2, NM, NB * NB)  2.23 us
    mul x2, other arithmetic, on_device(): return (electron.T * (norm / 55296.0), phonon * (norm / 24576.0))  1.89 us

profile of v5, /device:TPU:1, one launch (start us, length us, event | category | flops | bytes accessed | tf_op | source)
XLA Modules:
  0.0 87.2 jit_solution(4030710741526553937)
XLA Ops:
  0.6 2.2 %reshape.13.coup_ref = bf16[4,2,36,576]{3,2,1,0:T(8,128)(2,1)} reshape(bf16[4,2,20736]{2,1,0:T(2,128)(2,1)} %param.9) | data formatting | bytes 663552 | tf_op jit(solution)/shard_map/reshape | solution.py:436
  2.9 82.4 %linewidths.1 = (f32[24,32]{1,0:T(8,128)}, f32[4,36]{1,0:T(4,128)}) custom-call(s32[4,1024]{1,0:T(4,128)} %kq_ref.1, f32[4,36]{1,0:T(4,128)} %freq_ref.1, f32[3,1024]{1,0:T(4,128)} %bitcast.12, s32[3,64]{1,0:T(4,128)} %bitcast.14, bf16[4,2,36,576]{3,2,1,0:T(8,128)(2,1)} %reshape.13.coup_ref, bf16[36,4,36]{2,1,0:T(4,128)(2,1)} %bitcast.11, ...), custom_call_target="tpu_custom_call" | custom-call | tf_op jit(solution)/shard_map/linewidths/pallas_call | solution.py:411
  85.3 0.0 copy-start
  85.3 1.3 %multiply_bitcast_fusion = f32[32,24]{0,1:T(8,128)} fusion(f32[24,32]{1,0:T(8,128)} %get-tuple-element.4), kind=kLoop, calls=%fused_computation | loop fusion | flops 768 | bytes 6144 | tf_op jit(solution)/shard_map/mul | solution.py:440
  86.6 0.0 copy-done
  86.6 0.6 broadcast_multiply_fusion
Async XLA Ops:
  85.3 1.3 %copy-start = (f32[4,36]{1,0:T(4,128)S(1)}, f32[4,36]{1,0:T(4,128)}, u32[]{:S(2)}) copy-start(f32[4,36]{1,0:T(4,128)} %get-tuple-element.5) | copy-start | bytes 1732
